TPU v7x, 32 devices: a whole 2x2x4 slice. The times are simulated.
32 devices in a mesh: dp: 8 (over z, x), mp: 4 (over y, core).
Axes of the slice: x: 2, y: 2, z: 4, core: 2. Of those that a mesh axis runs over, the one named last changes fastest.
Arguments:
- inputs: bfloat16 [16384, 768], P('dp'), may hold values from -6 to 6
- segment_ids: int32 [32, 512], P('dp'), may hold values from 0 to 7, never falling along the last dimension, each value on 1 to 128 neighbouring positions
- cotangent: bfloat16 [16384, 768], P('dp'), may hold values from -6 to 6
- query_weight: bfloat16 [768, 768], P(None, 'mp'), may hold values from -0.3125 to 0.3125
- key_weight: bfloat16 [768, 768], P(None, 'mp'), may hold values from -0.21875 to 0.21875
- value_weight: bfloat16 [768, 768], P(None, 'mp'), may hold values from -0.21875 to 0.21875
- query_bias: float32 [768], P('mp'), may hold values from -3 to 3
- value_bias: float32 [768], P('mp'), may hold values from -3 to 3
- output_weight: bfloat16 [768, 768], P('mp'), may hold values from -0.875 to 0.875
- output_bias: float32 [768], replicated, may hold values from -3 to 3
- middle_gain: float32 [768], replicated, may hold values from 0.5 to 1.5
- middle_shift: float32 [768], replicated, may hold values from -3 to 3
- up_weight: bfloat16 [768, 3072], P(None, 'mp'), may hold values from -0.21875 to 0.21875
- up_bias: float32 [3072], P('mp'), may hold values from -3 to 3
- down_weight: bfloat16 [3072, 768], P('mp'), may hold values from -0.15625 to 0.15625
- down_bias: float32 [768], replicated, may hold values from -3 to 3
- final_gain: float32 [768], replicated, may hold values from 0.5 to 1.5
- final_shift: float32 [768], replicated, may hold values from -3 to 3
Outputs:
- layer_out: bfloat16 [16384, 768], P(('dp', 'mp'))
- input_grad: bfloat16 [16384, 768], P(('dp', 'mp'))
- grad_query_weight: float32 [768, 768], P(None, 'mp')
- grad_key_weight: float32 [768, 768], P(None, 'mp')
- grad_value_weight: float32 [768, 768], P(None, 'mp')
- grad_query_bias: float32 [768], P('mp')
- grad_value_bias: float32 [768], P('mp')
- grad_output_weight: float32 [768, 768], P('mp')
- grad_output_bias: float32 [768], replicated
- grad_middle_gain: float32 [768], replicated
- grad_middle_shift: float32 [768], replicated
- grad_up_weight: float32 [768, 3072], P(None, 'mp')
- grad_up_bias: float32 [3072], P('mp')
- grad_down_weight: float32 [3072, 768], P('mp')
- grad_down_bias: float32 [768], replicated
- grad_final_gain: float32 [768], replicated
- grad_final_shift: float32 [768], replicated
Inputs may be any that keep to these rules, and one draw needn't show every extreme that they name: `segment_ids`: in each row of 512 positions the passage numbers 0 to 7 appear in rising order, each on 1 to 128 consecutive positions, one on exactly 128.
All inputs are finite; a program needn't handle non-finite values.
Results may differ from a plain program's by a relative error of at most 0.025.
Values may be sent and summed in bfloat16 or wider, within the bound.
No kernel may reach another device: no remote copies, remote signals or barrier semaphores. Data moves between devices by JAX's collectives and lax.ppermute only.
A program may use at most 128 MiB of HBM per device.

v0:
```python
from functools import partial

import jax
import jax.numpy as jnp
from jax import lax
from jax.experimental import pallas as pl
from jax.experimental.pallas import tpu as pltpu
from jax.sharding import PartitionSpec as P

HEAD = 64
BAND = 128
EPSILON = 1e-12
ROOT_HALF = 0.7071067811865476
INV_ROOT_TAU = 0.3989422804014327
MASKED = -1e30
TAIL = 8
F32 = jnp.float32
BF16 = jnp.bfloat16
MIB = 1024 * 1024
SCALE = 4.0


def nn(a, b):
    return lax.dot_general(a, b, (((1,), (0,)), ((), ())), preferred_element_type=F32)


def nt(a, b):
    return lax.dot_general(a, b, (((1,), (1,)), ((), ())), preferred_element_type=F32)


def tn(a, b):
    return lax.dot_general(a, b, (((0,), (0,)), ((), ())), preferred_element_type=F32)


def window(block, seq):
    lo = max(block * BAND - BAND, 0)
    hi = min(block * BAND + 2 * BAND, seq)
    return lo, hi


def params(mib):
    return pltpu.CompilerParams(vmem_limit_bytes=mib * MIB)


def cost(us):
    return pl.CostEstimate(
        flops=int(us * SCALE * 1.15e9), bytes_accessed=int(us * SCALE * 3.6e6), transcendentals=0
    )


def whole(*shape):
    return pl.BlockSpec(shape, lambda *_: (0,) * len(shape), pipeline_mode=pl.Buffered(1))


def held(*shape):
    return pl.BlockSpec(shape, lambda *_: (0,) * len(shape))


def rows_of_heads(a):
    zero = jnp.zeros((HEAD, a.shape[1]), a.dtype)
    tiles = []
    for h in range(a.shape[0] // HEAD):
        mine = a[h * HEAD : (h + 1) * HEAD]
        if h % 2 == 0 and (h + 1) * HEAD == a.shape[0]:
            tiles.append(mine)
        else:
            tiles.append(jnp.concatenate([mine, zero] if h % 2 == 0 else [zero, mine], axis=0))
    return tiles


def tiles_of_heads(a):
    width = a.shape[1]
    return [a[:, h // 2 * 128 : min(h // 2 * 128 + 128, width)] for h in range(width // HEAD)]


def columns_of_heads(a):
    masked = []
    for h, tile in enumerate(tiles_of_heads(a)):
        if tile.shape[1] == HEAD:
            masked.append(tile)
        else:
            lane = lax.broadcasted_iota(jnp.int32, tile.shape, 1)
            masked.append(jnp.where((lane < HEAD) == (h % 2 == 0), tile, jnp.zeros_like(tile)))
    return masked


def store_tiles(ref, rows, per_head, scale=None):
    for at in range(0, len(per_head), 2):
        total = per_head[at] if at + 1 == len(per_head) else per_head[at] + per_head[at + 1]
        if scale is not None:
            total = total * scale
        lo = at * HEAD
        ref[rows, lo : lo + total.shape[1]] = total.astype(ref.dtype)


def attend_fwd_kernel(base, idx, x_ref, seg_ref, wq, wk, wv, wo, qb, vb,
                      q_ref, k_ref, v_ref, p_ref, ctx_ref, *parts):
    step = pl.program_id(0)
    seq = x_ref.shape[0]
    row = jnp.bitwise_xor(idx[0], base - step)
    x = x_ref[...]
    q = ((nt(x, wq[...]) + qb[...]).astype(BF16) * (HEAD**-0.5)).astype(BF16)
    k_t = nt(wk[...], x).astype(BF16)
    v = (nt(x, wv[...]) + vb[...]).astype(BF16)
    q_ref[0] = jnp.transpose(q)
    k_ref[0] = jnp.transpose(k_t)
    v_ref[0] = jnp.transpose(v)
    q_tiles, k_rows, v_cols = tiles_of_heads(q), rows_of_heads(k_t), columns_of_heads(v)
    heads = range(len(q_tiles))
    seg_row = seg_ref[pl.ds(row, 1), :]
    for i in range(seq // BAND):
        lo, hi = window(i, seq)
        rows = slice(i * BAND, (i + 1) * BAND)
        seg_k = jnp.broadcast_to(seg_row[:, lo:hi], (BAND, hi - lo))
        seg_q = jnp.transpose(jnp.broadcast_to(seg_row[:, rows], (BAND, BAND)))
        same = jnp.concatenate([seg_q] * ((hi - lo) // BAND), axis=1) == seg_k
        scores = [jnp.where(same, nn(q_tiles[h][rows], k_rows[h][:, lo:hi]), MASKED) for h in heads]
        tops = [jnp.max(a, axis=-1, keepdims=True) for a in scores]
        expos = [jnp.exp(a - m) for a, m in zip(scores, tops)]
        scales = [1.0 / jnp.sum(e, axis=-1, keepdims=True) for e in expos]
        probs = [(e * t).astype(BF16) for e, t in zip(expos, scales)]
        for h in heads:
            p_ref[0, h, rows, 0 : hi - lo] = probs[h]
        store_tiles(ctx_ref.at[0], rows, [nn(probs[h], v_cols[h][lo:hi]) for h in heads])
    part = nn(ctx_ref[0], wo[...]).astype(BF16)
    for j, ref in enumerate(parts):

        @pl.when(step == j)
        def _():
            ref[...] = part


def attend_fwd(base, count, idx, x, seg, wq, wk, wv, wo, qb, vb):
    seq = seg.shape[1]
    width, d = wq.shape
    heads = width // HEAD
    slot = lambda g, s: (g, 0, 0)
    natural = pl.BlockSpec((1, seq, width), slot)
    turned = pl.BlockSpec((1, width, seq), slot)
    saved = (
        jax.ShapeDtypeStruct((count, width, seq), BF16),
        jax.ShapeDtypeStruct((count, seq, width), BF16),
        jax.ShapeDtypeStruct((count, width, seq), BF16),
        jax.ShapeDtypeStruct((count, heads, seq, 3 * BAND), BF16),
        jax.ShapeDtypeStruct((count, seq, width), BF16),
    )
    args = (idx, x, seg, wq, wk, wv, wo, qb, vb)
    specs = [
        pl.BlockSpec((seq, d), lambda g, s: (jnp.bitwise_xor(s[0], base - g), 0)),
        whole(*seg.shape),
        whole(width, d),
        whole(width, d),
        whole(width, d),
        whole(width, d),
        whole(1, width),
        whole(1, width),
    ]
    return pl.pallas_call(
        partial(attend_fwd_kernel, base),
        out_shape=saved + (jax.ShapeDtypeStruct((seq, d), BF16),) * count,
        grid_spec=pltpu.PrefetchScalarGridSpec(
            num_scalar_prefetch=1,
            grid=(count,),
            in_specs=specs,
            out_specs=[
                turned,
                natural,
                turned,
                pl.BlockSpec((1, heads, seq, 3 * BAND), lambda g, s: (g, 0, 0, 0)),
                natural,
            ]
            + [held(seq, d)] * count,
        ),
        compiler_params=params(60 if base == 3 else 24),
        cost_estimate=cost(3.2 * count),
        name="attend_fwd",
    )(*args)


def gelu_parts(v):
    half = 0.5 * (1.0 + lax.erf(v * ROOT_HALF))
    return v * half, half + v * jnp.exp(-0.5 * v * v) * INV_ROOT_TAU


def by_rows(total, step, body, carry):
    def one(i, c):
        return body(pl.ds(pl.multiple_of(i * step, step), step), c)

    return lax.fori_loop(0, total // step, one, carry, unroll=2)


def fold(a):
    return jnp.sum(a.reshape(a.shape[0] // 8, 8, a.shape[1]), axis=0)


def up_kernel(
    idx, x_ref, pa, pb, pc, ob, gain, shift, u0, u1, u2, u3, b0, b1, b2, b3,
    hid, nrm, inv, low, act, slope,
):
    @pl.when(pl.program_id(0) == 0)
    def _():
        def body(rows, carry):
            middle = (
                pa[rows, :].astype(F32)
                + pb[rows, :].astype(F32)
                + pc[rows, :].astype(F32)
                + ob[...]
                + x_ref[rows, :].astype(F32)
            )
            centred = middle - jnp.mean(middle, axis=-1, keepdims=True)
            r = lax.rsqrt(jnp.mean(centred * centred, axis=-1, keepdims=True) + EPSILON)
            normed = centred * r
            hidden = normed * gain[...] + shift[...]
            nrm[rows, :] = normed
            inv[rows, :] = jnp.broadcast_to(r, (r.shape[0], 128))
            hid[rows, :] = hidden
            low[rows, :] = hidden.astype(BF16)
            return carry

        by_rows(low.shape[0], 64, body, 0)

    for r, (u, b) in enumerate(((u0, b0), (u1, b1), (u2, b2), (u3, b3))):
        value, deriv = gelu_parts(nn(low[...], u[...]) + b[...])
        act[r] = value.astype(BF16)
        slope[r] = deriv.astype(BF16)


def up(idx, x, own, recv, other, ob, gain, shift, us, bs):
    seq, d = other.shape
    units = us[0].shape[1]
    tile = 256
    row = pl.BlockSpec((seq, d), lambda n, s: (s[0], 0), pipeline_mode=pl.Buffered(1))
    wide = pl.BlockSpec((d, tile), lambda n, s: (0, n))
    bias = pl.BlockSpec((1, tile), lambda n, s: (0, n))
    out = pl.BlockSpec((4, seq, tile), lambda n, s: (0, 0, n))
    return pl.pallas_call(
        up_kernel,
        out_shape=(
            jax.ShapeDtypeStruct((seq, d), F32),
            jax.ShapeDtypeStruct((seq, d), F32),
            jax.ShapeDtypeStruct((seq, 128), F32),
            jax.ShapeDtypeStruct((seq, d), BF16),
            jax.ShapeDtypeStruct((4, seq, units), BF16),
            jax.ShapeDtypeStruct((4, seq, units), BF16),
        ),
        grid_spec=pltpu.PrefetchScalarGridSpec(
            num_scalar_prefetch=1,
            grid=(units // tile,),
            in_specs=[row] + [whole(seq, d)] * 3 + [whole(1, d)] * 3 + [wide] * 4 + [bias] * 4,
            out_specs=[held(seq, d), held(seq, d), held(seq, 128), held(seq, d), out, out],
        ),
        compiler_params=params(28),
        cost_estimate=cost(7.3),
        name="up",
    )(idx, x, own, recv, other, ob, gain, shift, *us, *bs)


def down_kernel(idx, act, d0, d1, d2, d3, hid, cot, db, gain, shift, out_ref, gf_ref, gl_ref, vec, acc):
    step = pl.program_id(0)
    total = None
    for r, w in enumerate((d0, d1, d2, d3)):
        term = nn(act[r], w[...])
        total = term if total is None else total + term
    acc[step] = total

    @pl.when(step == pl.num_programs(0) - 1)
    def _():
        def body(rows, carry):
            parts = [acc[n, rows, :] for n in range(acc.shape[0])]
            final = jnp.concatenate(parts, axis=1) + db[...] + hid[rows, :]
            centred = final - jnp.mean(final, axis=-1, keepdims=True)
            r = lax.rsqrt(jnp.mean(centred * centred, axis=-1, keepdims=True) + EPSILON)
            normed = centred * r
            out_ref[rows, :] = (normed * gain[...] + shift[...]).astype(BF16)
            cv = cot[rows, :].astype(F32)
            c = cv * gain[...]
            grad = r * (
                c
                - jnp.mean(c, axis=-1, keepdims=True)
                - normed * jnp.mean(c * normed, axis=-1, keepdims=True)
            )
            gf_ref[rows, :] = grad
            gl_ref[rows, :] = grad.astype(BF16)
            return tuple(a + b for a, b in zip(carry, (fold(cv * normed), fold(cv), fold(grad))))

        zero = jnp.zeros((8, hid.shape[1]), F32)
        sums = by_rows(hid.shape[0], 64, body, (zero, zero, zero))
        vec[...] = jnp.zeros_like(vec)
        for j, total in enumerate(sums):
            vec[j : j + 1, :] = jnp.sum(total, axis=0, keepdims=True)


def down(idx, act, ds, hid, cot, db, gain, shift):
    seq, d = hid.shape
    units = act.shape[2]
    tile = 256
    wide = pl.BlockSpec((units, tile), lambda n, s: (0, n))
    row = pl.BlockSpec((seq, d), lambda n, s: (s[0], 0), pipeline_mode=pl.Buffered(1))
    return pl.pallas_call(
        down_kernel,
        out_shape=(
            jax.ShapeDtypeStruct((seq, d), BF16),
            jax.ShapeDtypeStruct((seq, d), F32),
            jax.ShapeDtypeStruct((seq, d), BF16),
            jax.ShapeDtypeStruct((8, d), F32),
        ),
        grid_spec=pltpu.PrefetchScalarGridSpec(
            num_scalar_prefetch=1,
            grid=(d // tile,),
            in_specs=[whole(4, seq, units)] + [wide] * 4 + [whole(seq, d), row] + [whole(1, d)] * 3,
            out_specs=[held(seq, d), held(seq, d), held(seq, d), held(8, d)],
            scratch_shapes=[pltpu.VMEM((d // tile, seq, tile), F32)],
        ),
        compiler_params=params(24),
        cost_estimate=cost(6.2),
        name="down",
    )(idx, act, *ds, hid, cot, db, gain, shift)


def back_kernel(
    gl, slope, d0, d1, d2, d3, u0, u1, u2, u3, gf, nrm, inv, gain, vecf, gp, gm_ref, gml_ref, vec, acc
):
    step = pl.program_id(0)
    tile = slope.shape[2]
    total = None
    for r, (w_d, w_u) in enumerate(((d0, u0), (d1, u1), (d2, u2), (d3, u3))):
        pre = (nt(gl[...], w_d[...]) * slope[r].astype(F32)).astype(BF16)
        gp[r] = pre
        sums = jnp.sum(pre.astype(F32), axis=0, keepdims=True)
        vec[r : r + 1, pl.ds(pl.multiple_of(step * tile, tile), tile)] = sums
        term = nt(pre, w_u[...])
        total = term if total is None else total + term

    @pl.when(step == 0)
    def _():
        acc[...] = total

    @pl.when(step > 0)
    def _():
        acc[...] += total

    @pl.when(step == pl.num_programs(0) - 1)
    def _():
        def body(rows, carry):
            grad = acc[rows, :] + gf[rows, :]
            normed = nrm[rows, :]
            c = grad * gain[...]
            gm = inv[rows, 0:1] * (
                c
                - jnp.mean(c, axis=-1, keepdims=True)
                - normed * jnp.mean(c * normed, axis=-1, keepdims=True)
            )
            gm_ref[rows, :] = gm
            gml_ref[rows, :] = gm.astype(BF16)
            return tuple(a + b for a, b in zip(carry, (fold(grad * normed), fold(grad), fold(gm))))

        zero = jnp.zeros((8, gf.shape[1]), F32)
        sums = by_rows(gf.shape[0], 64, body, (zero, zero, zero))
        for j, total in enumerate(sums):
            vec[4 + j : 5 + j, :] = jnp.sum(total, axis=0, keepdims=True)
        vec[7:10, :] = vecf[0:3, :]
        vec[10:16, :] = jnp.zeros((6, gf.shape[1]), F32)


def back(gl, slope, ds, us, gf, nrm, inv, gain, vecf):
    seq, d = gf.shape
    units = slope.shape[2]
    tile = 256
    tall = pl.BlockSpec((4, seq, tile), lambda n: (0, 0, n))
    w_d = pl.BlockSpec((tile, d), lambda n: (n, 0))
    w_u = pl.BlockSpec((d, tile), lambda n: (0, n))
    return pl.pallas_call(
        back_kernel,
        out_shape=(
            jax.ShapeDtypeStruct((4, seq, units), BF16),
            jax.ShapeDtypeStruct((seq, d), F32),
            jax.ShapeDtypeStruct((seq, d), BF16),
            jax.ShapeDtypeStruct((16, d), F32),
        ),
        grid=(units // tile,),
        in_specs=[whole(seq, d), tall]
        + [w_d] * 4
        + [w_u] * 4
        + [whole(seq, d), whole(seq, d), whole(seq, 128), whole(1, d), whole(8, d)],
        out_specs=[tall, held(seq, d), held(seq, d), held(16, d)],
        scratch_shapes=[pltpu.VMEM((seq, d), F32)],
        compiler_params=params(28),
        cost_estimate=cost(10.8),
        name="back",
    )(gl, slope, *ds, *us, gf, nrm, inv, gain, vecf)


def place(idx, e, z_major=False):
    first, second = (idx[2], idx[1]) if z_major else (idx[1], idx[2])
    return jnp.bitwise_xor(e // 2, first) * 2 + jnp.bitwise_xor(e % 2, second)


def spread(idx, value, put, z_major=False):
    size = value.shape[0] // 4
    for e in range(4):
        put(place(idx, e, z_major), size, value[e * size : (e + 1) * size])


def slot_rows(slot, size):
    return pl.ds(pl.multiple_of(slot * size, 8), size)


def put_halves(first, second):
    def put(slot, size, piece):
        @pl.when(slot < 2)
        def _():
            first[slot_rows(slot, size), :] = piece.astype(BF16)

        @pl.when(slot >= 2)
        def _():
            second[slot_rows(slot - 2, size), :] = piece.astype(BF16)

    return put


def outer_kernel(flip, z_major, halves, idx, left, varied, out, *kept):
    step = pl.program_id(0)
    value = tn(varied[0], left[...]) if flip else tn(left[...], varied[0])

    def whole_to(ref):
        def put(slot, size, piece):
            ref[slot_rows(slot, size), :] = piece.astype(BF16)

        return put

    @pl.when(step < 2)
    def _():
        spread(idx, value, whole_to(out.at[step]), z_major)

    if not halves:
        first, second = kept

        @pl.when(step >= 2)
        def _():
            spread(idx, value, put_halves(first.at[step - 2], second.at[step - 2]), z_major)

    else:
        far_left, near_first, near_second, first, second = kept
        n = far_left.shape[1]

        @pl.when(step >= 2)
        def _():
            spread(idx, value[:, n:], put_halves(first.at[step - 2], second.at[step - 2]), z_major)

        @pl.when(step == 2)
        def _():
            spread(idx, value[:, :n], whole_to(far_left), z_major)

        @pl.when(step == 3)
        def _():
            spread(idx, value[:, :n], put_halves(near_first, near_second), z_major)


def outer(flip, z_major, halves, idx, left, varied):
    seq, d = left.shape
    units = varied.shape[2]
    rows, cols = (units, d) if flip else (d, units)
    shapes = [(2, rows, cols)]
    if halves:
        cols = cols // 2
        shapes += [(rows, cols), (rows // 2, cols), (rows // 2, cols)]
    shapes += [(2, rows // 2, cols), (2, rows // 2, cols)]
    member = lambda g, s: (jnp.where(g < 2, 3 - 2 * g, 6 - 2 * g), 0, 0)
    return pl.pallas_call(
        partial(outer_kernel, flip, z_major, halves),
        out_shape=[jax.ShapeDtypeStruct(a, BF16) for a in shapes],
        grid_spec=pltpu.PrefetchScalarGridSpec(
            num_scalar_prefetch=1,
            grid=(4,),
            in_specs=[whole(seq, d), pl.BlockSpec((1, seq, units), member)],
            out_specs=[whole(*a) for a in shapes],
        ),
        compiler_params=params(20),
        cost_estimate=cost(5.5),
        name="outer",
    )(idx, left, varied)


def attend_bwd_kernel(count, later, last, idx, x_ref, *rest):
    gmls, rest = rest[:count], rest[count:]
    q_ref, k_ref, v_ref, p_ref, ctx_ref, wq, wk, wv, wo = rest[:9]
    rest = rest[9:]
    if later:
        before, vec_before = rest[:2]
        rest = rest[2:]
    if last:
        shared, shared_y = rest[:2]
        rest = rest[2:]
    parts, rest = rest[:count], rest[count:]
    if last:
        first, second, tail, vec, grads, gq_s, gk_s, gv_s = rest
    else:
        grads, vec, gq_s, gk_s, gv_s = rest
    step = pl.program_id(0)
    seq = x_ref.shape[0]
    width = wq.shape[0]
    blocks = seq // BAND

    @pl.when(step == 0)
    def _():
        if later:
            grads[...] = before[...]
            vec[...] = vec_before[...]
        else:
            grads[...] = jnp.zeros_like(grads)
            vec[...] = jnp.zeros_like(vec)

    gml = gmls[0][...] if count == 1 else jnp.where(step == 0, gmls[0][...], gmls[1][...])
    x, ctx, q_t, k = x_ref[...], ctx_ref[0], q_ref[0], k_ref[0]
    gctx = nt(gml, wo[...]).astype(BF16)
    gctx_t = jnp.transpose(gctx)
    g_tiles, v_rows, k_cols = tiles_of_heads(gctx), rows_of_heads(v_ref[0]), columns_of_heads(k)
    heads = range(len(g_tiles))
    gk = [[None] * blocks for _ in heads]
    gv = [[None] * blocks for _ in heads]
    for i in range(blocks):
        lo, hi = window(i, seq)
        rows = slice(i * BAND, (i + 1) * BAND)
        probs_low = [p_ref[0, h, rows, 0 : hi - lo] for h in heads]
        gprobs = [nn(g_tiles[h][rows], v_rows[h][:, lo:hi]) for h in heads]
        probs = [p.astype(F32) for p in probs_low]
        dots = [jnp.sum(a * b, axis=-1, keepdims=True) for a, b in zip(gprobs, probs)]
        gscores = [(p * (g - t)).astype(BF16) for g, p, t in zip(gprobs, probs, dots)]
        store_tiles(gq_s, rows, [nn(gscores[h], k_cols[h][lo:hi]) for h in heads], HEAD**-0.5)
        for h in heads:
            mine = slice(h * HEAD, (h + 1) * HEAD)
            gk_i = nn(q_t[mine, rows], gscores[h])
            gv_i = nn(gctx_t[mine, rows], probs_low[h])
            for j in range(lo // BAND, hi // BAND):
                at = slice(j * BAND - lo, (j + 1) * BAND - lo)
                gk[h][j] = gk_i[:, at] if gk[h][j] is None else gk[h][j] + gk_i[:, at]
                gv[h][j] = gv_i[:, at] if gv[h][j] is None else gv[h][j] + gv_i[:, at]
    for h in heads:
        mine = slice(h * HEAD, (h + 1) * HEAD)
        for j in range(blocks):
            cols = slice(j * BAND, (j + 1) * BAND)
            gk_s[mine, cols] = gk[h][j].astype(BF16)
            gv_s[mine, cols] = gv[h][j].astype(BF16)
    gq, gk_t, gv_t = gq_s[...], gk_s[...], gv_s[...]
    gv_n = jnp.transpose(gv_t)
    grads[0:width] += tn(gq, x)
    grads[width : 2 * width] += nn(gk_t, x)
    grads[2 * width : 3 * width] += nn(gv_t, x)
    grads[3 * width : 4 * width] += tn(ctx, gml)
    vec[0:1, 0:width] += jnp.sum(gq.astype(F32), axis=0, keepdims=True)
    vec[1:2, 0:width] += jnp.sum(gv_n.astype(F32), axis=0, keepdims=True)
    part = (nn(gq, wq[...]) + nn(jnp.transpose(gk_t), wk[...]) + nn(gv_n, wv[...])).astype(BF16)

    for j, ref in enumerate(parts):

        @pl.when(step == j)
        def _():
            ref[...] = part

    if last:

        @pl.when(step == count - 1)
        def _():
            tail[...] = jnp.zeros_like(tail)
            tail[0:1, :] = shared[0:1, :] + shared_y[2:3, :]
            for j in range(6):
                at = TAIL * ((j + 1) // 3) + (j + 1) % 3
                tail[at : at + 1, :] = shared[4 + j : 5 + j, :] + shared_y[4 + j : 5 + j, :]
            tail[2 * TAIL + 1 : 2 * TAIL + 3, :] = vec[0:2, :]
            for e in range(4):
                body = grads[e * width : (e + 1) * width]
                both = jnp.concatenate([body, tail[e * TAIL : (e + 1) * TAIL]], axis=0)
                put_halves(first, second)(place(idx, e), width + TAIL, both)


def attend_bwd(base, last, idx, x, gmls, kept, wq, wk, wv, wo, before=None, shared=()):
    q, k, v, p, ctx = kept
    width, d = wq.shape
    seq = gmls[0].shape[0]
    heads = width // HEAD
    count = len(gmls)
    later = before is not None
    slot = lambda g, s: (count - 1 - g, 0, 0)
    natural = pl.BlockSpec((1, seq, width), slot)
    turned = pl.BlockSpec((1, width, seq), slot)
    specs = [
        pl.BlockSpec((seq, d), lambda g, s: (jnp.bitwise_xor(s[0], base + g), 0)),
    ] + [whole(seq, d)] * count + [
        turned,
        natural,
        turned,
        pl.BlockSpec((1, heads, seq, 3 * BAND), lambda g, s: (count - 1 - g, 0, 0, 0)),
        natural,
    ] + [whole(width, d)] * 4
    args = (idx, x, *gmls, q, k, v, p, ctx, wq, wk, wv, wo)
    part = jax.ShapeDtypeStruct((seq, d), BF16)
    small = jax.ShapeDtypeStruct((8, d), F32)
    scratch = [
        pltpu.VMEM((seq, width), BF16),
        pltpu.VMEM((width, seq), BF16),
        pltpu.VMEM((width, seq), BF16),
    ]
    if later:
        specs += [whole(4 * width, d), whole(8, d)]
        args += tuple(before)
    if last:
        specs += [whole(16, d)] * 2
        args += tuple(shared)
        half = 2 * (width + TAIL)
        shapes = (part,) * count + (jax.ShapeDtypeStruct((half, d), BF16),) * 2
        outs = [held(seq, d)] * count + [held(half, d)] * 2
        scratch = [
            pltpu.VMEM((4 * TAIL, d), F32), pltpu.VMEM((8, d), F32), pltpu.VMEM((4 * width, d), F32)
        ] + scratch
    else:
        shapes = (part,) * count + (jax.ShapeDtypeStruct((4 * width, d), F32), small)
        outs = [held(seq, d)] * count + [held(4 * width, d), held(8, d)]
    return pl.pallas_call(
        partial(attend_bwd_kernel, count, later, last),
        out_shape=shapes,
        grid_spec=pltpu.PrefetchScalarGridSpec(
            num_scalar_prefetch=1, grid=(count,), in_specs=specs, out_specs=outs, scratch_shapes=scratch
        ),
        compiler_params=params(28),
        cost_estimate=cost(5.0 if later else 10.0),
        name="attend_bwd",
    )(*args)


def join_kernel(idx, *refs):
    pieces, outs = refs[:-2], refs[-2:]
    rows = pieces[0].shape[0]
    for j, piece in enumerate(pieces):
        at = place(idx, j % 4)
        outs[j // 4][slot_rows(at, rows), :] = piece[...]


def join(idx, *pieces):
    rows, d = pieces[0].shape
    return pl.pallas_call(
        join_kernel,
        out_shape=[jax.ShapeDtypeStruct((4 * rows, d), BF16)] * 2,
        grid_spec=pltpu.PrefetchScalarGridSpec(
            num_scalar_prefetch=1,
            grid=(1,),
            in_specs=[whole(rows, d)] * 8,
            out_specs=[whole(4 * rows, d)] * 2,
        ),
        compiler_params=params(8),
        cost_estimate=cost(1.0),
        name="join",
    )(idx, *pieces)


def unpack_kernel(z_major, given, tail, idx, *refs):
    pieces, outs = refs[:given], refs[given:]
    size = pieces[0].shape[0] * given // 4
    body = size - tail
    for slot in range(4):
        piece = pieces[slot][...] if given == 4 else pieces[0][slot * size : (slot + 1) * size]
        at = place(idx, slot, z_major)
        if not tail:
            outs[0][slot_rows(at, size), :] = piece.astype(F32)
        else:
            outs[4][slot_rows(at, tail), :] = piece[body:].astype(F32)
            for j in range(4):

                @pl.when(at == j)
                def _():
                    outs[j][...] = piece[:body].astype(F32)


def unpack(idx, z_major, tail, pieces):
    d = pieces[0].shape[1]
    total = sum(p.shape[0] for p in pieces)
    shapes = [(total // 4 - tail, d)] * 4 + [(4 * tail, d)] if tail else [(total, d)]
    return pl.pallas_call(
        partial(unpack_kernel, z_major, len(pieces), tail),
        out_shape=[jax.ShapeDtypeStruct(a, F32) for a in shapes],
        grid_spec=pltpu.PrefetchScalarGridSpec(
            num_scalar_prefetch=1,
            grid=(1,),
            in_specs=[whole(*p.shape) for p in pieces],
            out_specs=[whole(*a) for a in shapes],
        ),
        compiler_params=params(10),
        cost_estimate=cost(0.0),
        name="unpack",
    )(idx, *pieces)


def mix_kernel(order, v, r, out):
    for j, other in enumerate(order):
        out[j : j + 1, :] = v[j : j + 1, :] + r[other : other + 1, :]
    out[len(order) :, :] = v[len(order) :, :] + r[len(order) :, :]


def small(kernel, *arrays):
    return pl.pallas_call(
        kernel,
        out_shape=jax.ShapeDtypeStruct(arrays[0].shape, F32),
        compiler_params=params(4),
        cost_estimate=cost(0.5),
        name="small",
    )(*arrays)


def block(array, *index, rows=None, cols=None):
    (r, n_r), (c, n_c) = rows or (0, 1), cols or (0, 1)
    shape = (1,) * len(index) + (array.shape[-2] // n_r, array.shape[-1] // n_c)
    return array, shape, index + (r, c)


def add_up_kernel(sizes, idx, *refs):
    outs = refs[sum(sizes) :]
    col = 0
    for size in sizes:
        total = None
        for ref in refs[:size]:
            piece = ref[...]
            piece = piece.reshape(piece.shape[-2:]).astype(F32)
            total = piece if total is None else total + piece
        refs = refs[size:]
        cols = slice(col, col + total.shape[1])
        col += total.shape[1]
        n = outs[0].shape[0]
        for j, out in enumerate(outs):
            out[:, cols] = total[j * n : (j + 1) * n].astype(BF16)


def add_up(idx, pieces, *parts):
    blocks = [b for part in parts for b in part]
    rows = blocks[0][1][-2] // pieces
    cols = sum(part[0][1][-1] for part in parts)
    out = pl.pallas_call(
        partial(add_up_kernel, tuple(len(part) for part in parts)),
        out_shape=[jax.ShapeDtypeStruct((rows, cols), BF16)] * pieces,
        grid_spec=pltpu.PrefetchScalarGridSpec(
            num_scalar_prefetch=1,
            grid=(1,),
            in_specs=[
                pl.BlockSpec(b[1], partial(lambda at, g, s: at, b[2]), pipeline_mode=pl.Buffered(1))
                for b in blocks
            ],
            out_specs=[whole(rows, cols)] * pieces,
        ),
        compiler_params=params(12),
        cost_estimate=cost(0.02),
        name="add_up",
    )(idx, *(b[0] for b in blocks))
    return out if pieces > 1 else out[0]


def finish_kernel(idx, a, b, c, gm, out):
    total = a[...].astype(F32) + b[...].astype(F32) + c[...].astype(F32) + gm[...]
    out[...] = total.astype(BF16)


def finish(idx, a, b, c, gm):
    seq, d = a.shape
    part = pl.BlockSpec((seq // 4, d), lambda n, s: (n, 0))
    return pl.pallas_call(
        finish_kernel,
        out_shape=jax.ShapeDtypeStruct((seq, d), BF16),
        grid_spec=pltpu.PrefetchScalarGridSpec(
            num_scalar_prefetch=1, grid=(4,), in_specs=[part] * 4, out_specs=part
        ),
        compiler_params=params(8),
        cost_estimate=cost(0.0),
        name="finish",
    )(idx, a, b, c, gm)


def over(name, bit):
    size = lax.axis_size(name)
    pairs = [(i, i ^ bit) for i in range(size)]
    return lambda a: lax.ppermute(a, name, pairs)


class Order:
    def __init__(self):
        self.last = ()

    def then(self, a):
        return lax.optimization_barrier((a, self.last))[0]

    def done(self, out):
        self.last = (jax.tree.leaves(out)[-1],)
        return out

    def wait(self, *arrays):
        arrays = self.then(arrays)
        self.last = self.last + tuple(arrays)
        return arrays


def local(
    inputs, segment_ids, cotangent, query_weight, key_weight, value_weight, query_bias, value_bias,
    output_weight, output_bias, middle_gain, middle_shift, up_weight, up_bias, down_weight, down_bias,
    final_gain, final_shift,
):
    rows_here, seq = segment_ids.shape
    members = lax.axis_size("mp")
    assert members == 4 and rows_here == 4
    staged = lax.axis_size("dp") == 8
    me = lax.axis_index("mp")
    spot = lax.axis_index("dp")
    x_bit = jnp.bitwise_and(spot, 1) if staged else 0 * spot
    z_bit = jnp.bitwise_and(jnp.right_shift(spot, 1), 1) if staged else 0 * spot
    idx = jnp.stack([me, x_bit, z_bit]).astype(jnp.int32)
    core, y, both = over("mp", 1), over("mp", 2), over("mp", 3)
    x, z1, z2 = over("dp", 1), over("dp", 2), over("dp", 4)
    line = lambda v: v.reshape(1, -1)
    in_hbm = lambda a: pltpu.with_memory_space_constraint(a, pltpu.HBM)
    inputs, cotangent = in_hbm(inputs), in_hbm(cotangent)
    order = Order()
    then, done, wait = order.then, order.done, order.wait
    kernel = lambda f, *a: done(f(then(idx), *a))

    if staged:
        quarter = up_weight.shape[0] // 4
        at = (x_bit * 2 + z_bit) * quarter
        mine = [lax.dynamic_slice_in_dim(w, at, quarter, 0) for w in (up_weight, down_weight)]
        mine = done(mine)
        near_u, near_d = y(mine[0]), y(mine[1])
    u1, d1 = core(up_weight), core(down_weight)
    ub = line(up_bias)
    ub1, ub2 = core(ub), y(ub)

    weights = (query_weight.T, key_weight.T, value_weight.T, output_weight)
    fwd = (inputs, segment_ids) + weights + (line(query_bias), line(value_bias))
    *kept3, part3 = kernel(partial(attend_fwd, 3, 1), *fwd)
    from3 = core(part3)
    if staged:
        (near_u,) = wait(near_u)
        x_u, z_u = x(near_u), z1(near_u)
    *kept2, part2 = kernel(partial(attend_fwd, 2, 1), *fwd)
    if staged:
        (near_d,) = wait(near_d)
        x_d, z_d = x(near_d), z1(near_d)
    u1, d1, ub1, ub2 = wait(u1, d1, ub1, ub2)
    ub3 = core(ub2)
    other = y(done(part2 + then(from3)))
    if staged:
        x_u, z_u = wait(x_u, z_u)
        far_u = z1(x_u)
    *kept10, part1, part0 = kernel(partial(attend_fwd, 1, 2), *fwd)
    from1 = core(part1)
    if staged:
        z_d, x_d, ub3 = wait(z_d, x_d, ub3)
        far_d = x(z_d)
        (other,) = wait(other)
        far_u, far_d = wait(far_u, far_d)
        u2, d2 = kernel(join, near_u, z_u, x_u, far_u, near_d, z_d, x_d, far_d)
        u3, d3 = core(u2), core(d2)
    else:
        u2, u3, d2, d3 = y(up_weight), both(up_weight), y(down_weight), both(down_weight)
    us = (up_weight, u1, u2, u3)
    ds = (down_weight, d1, d2, d3)
    hidden, normed, inverse, low, act, slope = kernel(
        up, inputs, part0, from1, other, line(output_bias), line(middle_gain), line(middle_shift),
        us, (ub, ub1, ub2, ub3),
    )
    layer_out, grad_final, grad_low, vec_fin = kernel(
        down, act, ds, hidden, cotangent, line(down_bias), line(final_gain), line(final_shift)
    )

    gd31, first_d, second_d = kernel(partial(outer, True, False, False), grad_low, act)
    rd = core(gd31)
    gp, grad_mid, mid0, vec = done(
        back(grad_low, slope, ds, us, grad_final, normed, inverse, then(line(middle_gain)), vec_fin)
    )
    mid2, mid1 = y(mid0), core(mid0)
    vec_core = core(vec)
    half = first_d.shape[1]
    rd = then(rd)
    second_d = done(second_d + rd[:, half:])
    got_d = x(second_d) if staged else None
    gu31, far_l, near_l1, near_l2, first_r, second_r = kernel(
        partial(outer, False, True, True), low, gp
    )
    ru = core(gu31)
    in0, in1, *before = kernel(partial(attend_bwd, 0, False), inputs, (mid0, mid1), kept10, *weights)
    from_in1 = core(in1)
    n = far_l.shape[1]
    ru = then(ru)
    second_r = second_r + ru[:, half:, n:]
    far_l = done(far_l + ru[0, :, :n])
    got_r = z1(second_r) if staged else None
    got_l = y(far_l)
    (mid2,) = wait(mid2)
    mid3 = core(mid2)
    vec = done(small(partial(mix_kernel, (1, 0, 3, 2)), vec, then(vec_core)))
    vec_y = y(vec)
    in2, *before = kernel(partial(attend_bwd, 2, False), inputs, (mid2,), kept2, *weights, before)
    (vec_y,) = wait(vec_y)
    in3, first_a, second_a = kernel(
        partial(attend_bwd, 3, True), inputs, (mid3,), kept3, *weights, before, (vec, vec_y)
    )
    width = query_bias.shape[0]

    if staged:
        top = dict(rows=(0, 2))
        left, right = dict(cols=(0, 2)), dict(cols=(1, 2))
        got_a = x(second_a)
        from_in3 = core(in3)
        more_d = y(
            kernel(add_up, 1, [block(first_d, 0), block(rd, 0, **top), block(got_d, 0)])
        )
        more_r = y(
            kernel(add_up, 1, [block(first_r, 0), block(ru, 0, **top, **right), block(got_r, 0)])
        )
        more_l = z1(
            kernel(
                add_up, 1,
                [block(near_l2), block(ru, 1, rows=(1, 2), **left), block(got_l, rows=(1, 2))],
            )
        )
        keep_a, send_a = kernel(add_up, 2, [block(first_a), block(got_a)])
        got_a = z1(send_a)
        keep_d, send_d = kernel(
            add_up, 2, [block(first_d, 1), block(rd, 1, **top), block(got_d, 1), block(more_d)]
        )
        got_d = z1(send_d)
        keep_u, send_u = kernel(
            add_up, 2,
            [block(near_l1), block(ru, 1, **top, **left), block(got_l, **top), block(more_l)],
            [block(first_r, 1), block(ru, 1, **top, **right), block(got_r, 1), block(more_r)],
        )
        got_u = x(send_u)
        from_in2 = y(kernel(add_up, 1, [block(in2), block(from_in3)]))
        s_a = kernel(add_up, 1, [block(keep_a), block(got_a)])
        got_a = z2(s_a)
        s_d = kernel(add_up, 1, [block(keep_d), block(got_d)])
        got_d = z2(s_d)
        s_u = kernel(add_up, 1, [block(keep_u), block(got_u)])
        got_u = z2(s_u)
        s_a = kernel(add_up, 1, [block(s_a), block(got_a)])
        q_a, p_a = z1(s_a), x(s_a)
        input_grad = kernel(finish, in0, from_in1, from_in2, grad_mid)
        (q_a,) = wait(q_a)
        r_a = x(q_a)
        s_d = kernel(add_up, 1, [block(s_d), block(got_d)])
        q_d, p_d = z1(s_d), x(s_d)
        s_u = kernel(add_up, 1, [block(s_u), block(got_u)])
        q_u, p_u = x(s_u), z1(s_u)
        (q_d,) = wait(q_d)
        r_d = x(q_d)
        grad_q, grad_k, grad_v, grad_o, vecs = kernel(unpack, False, TAIL, (s_a, q_a, p_a, r_a))
        (q_u,) = wait(q_u)
        r_u = z1(q_u)
        (grad_down,) = kernel(unpack, False, 0, (s_d, q_d, p_d, r_d))
        (grad_up,) = kernel(unpack, True, 0, (s_u, q_u, p_u, r_u))
    else:
        input_grad = finish(idx, in0, from_in1, y(in2 + core(in3)), grad_mid)
        td = jnp.concatenate([first_d[1] + rd[1, :half], second_d[1]]) + y(
            jnp.concatenate([first_d[0] + rd[0, :half], second_d[0]])
        )
        tl = jnp.concatenate([near_l1, near_l2]) + ru[1, :, :n] + got_l
        tr = jnp.concatenate([first_r[1] + ru[1, :half, n:], second_r[1]]) + y(
            jnp.concatenate([first_r[0] + ru[0, :half, n:], second_r[0]])
        )
        tu = jnp.concatenate([tl, tr], axis=1)
        ta = jnp.concatenate([first_a, second_a])
        td, tu, ta = lax.psum((td, tu, ta), "dp")
        (grad_down,) = unpack(idx, False, 0, (td,))
        (grad_up,) = unpack(idx, True, 0, (tu,))
        grad_q, grad_k, grad_v, grad_o, vecs = unpack(idx, False, TAIL, (ta,))

    bias_up, gain_mid, shift_mid, bias_out, gain_fin, shift_fin, bias_down, bias_q, bias_v = (
        vecs[TAIL * (j // 3) + j % 3] for j in range(9)
    )
    return (
        layer_out, input_grad, grad_q.T, grad_k.T, grad_v.T, bias_q[:width], bias_v[:width], grad_o,
        bias_out, gain_mid, shift_mid, grad_up, bias_up, grad_down, bias_down, gain_fin, shift_fin,
    )


def solution(mesh):
    tokens = P("dp", None)
    columns, units, stacked, full = P(None, "mp"), P("mp"), P("mp", None), P()
    shared = P(("dp", "mp"), None)
    placed = (
        tokens, tokens, tokens, columns, columns, columns, units, units, stacked, full, full, full,
        columns, units, stacked, full, full, full,
    )
    given = (
        shared, shared, columns, columns, columns, units, units, stacked, full, full, full,
        columns, units, stacked, full, full, full,
    )
    return jax.shard_map(local, mesh=mesh, in_specs=placed, out_specs=given, check_vma=False)
```

profile of v0, /device:TPU:0, one launch (start us, length us, event | category | flops | bytes accessed | tf_op | source)
XLA Modules:
  0.0 218.9 jit_solution(15873305852385945536)
XLA Ops:
  10.9 6.3 %attend_fwd.3 = (bf16[1,192,512]{2,1,0:T(8,128)(2,1)}, bf16[1,512,192]{2,1,0:T(8,128)(2,1)}, bf16[1,192,512]{2,1,0:T(8,128)(2,1)}, bf16[1,3,512,384]{3,2,1,0:T(8...) custom-call(s32[3]{0:T(128)} %pad_add_fusion.idx, bf16[2048,768]{1,0:T(8,128)(2,1)} %x_ref.13, ...), custom_call_target="tpu_custom_call" | custom-call | flops 14720000000 | bytes 46080000 | tf_op jit(solution)/shard_map/attend_fwd/pallas_call | solution.py:158
  23.6 4.5 %attend_fwd.4 = (bf16[1,192,512]{2,1,0:T(8,128)(2,1)S(1)}, bf16[1,512,192]{2,1,0:T(8,128)(2,1)S(1)}, bf16[1,192,512]{2,1,0:T(8,128)(2,1)S(1)}, bf16[1,3,512,384]...) custom-call(s32[3]{0:T(128)S(1)} %copy-done, bf16[2048,768]{1,0:T(8,128)(2,1)} %x_ref.13, ...), custom_call_target="tpu_custom_call" | custom-call | flops 14720000000 | bytes 46080000 | tf_op jit(solution)/shard_map/attend_fwd/pallas_call | solution.py:158
  31.9 7.7 %attend_fwd.5 = (bf16[2,192,512]{2,1,0:T(8,128)(2,1)S(1)}, bf16[2,512,192]{2,1,0:T(8,128)(2,1)S(1)}, bf16[2,192,512]{2,1,0:T(8,128)(2,1)S(1)}, bf16[2,3,512,384]...) custom-call(s32[3]{0:T(128)S(1)} %copy-done, ...), custom_call_target="tpu_custom_call" | custom-call | flops 29440000000 | bytes 92160000 | tf_op jit(solution)/shard_map/attend_fwd/pallas_call | solution.py:158
  42.3 8.3 %collective-permute-done.12.pc = bf16[512,768]{1,0:T(8,128)(2,1)S(1)} collective-permute-done((bf16[512,768]{1,0:T(8,128)(2,1)S(1)}, bf16[512,768]{1,0:T(8,128)(2,1)S(1)}, u32[]{:S(2)}, u32[]{:S(2)}) %collective-permute-start.12) | collective-permute-done | bytes 786464 | tf_op jit(solution)/shard_map/ppermute | solution.py:777
  53.1 3.2 %collective-permute-done.15.pb = bf16[512,768]{1,0:T(8,128)(2,1)S(1)} collective-permute-done((bf16[512,768]{1,0:T(8,128)(2,1)S(1)}, bf16[512,768]{1,0:T(8,128)(2,1)S(1)}, u32[]{:S(2)}, u32[]{:S(2)}) %collective-permute-start.15) | collective-permute-done | bytes 786464 | tf_op jit(solution)/shard_map/ppermute | solution.py:777
  56.4 8.5 %up.1 = (f32[512,768]{1,0:T(8,128)S(1)}, f32[512,768]{1,0:T(8,128)S(1)}, f32[512,128]{1,0:T(8,128)S(1)}, bf16[512,768]{1,0:T(8,128)(2,1)S(1)}, bf16[4,512,768]{2...) custom-call(s32[3]{0:T(128)S(1)} %copy-done, bf16[2048,768]{1,0:T(8,128)(2,1)} %x_ref.13, ...), custom_call_target="tpu_custom_call" | custom-call | flops 33579999232 | bytes 105120000 | tf_op jit(solution)/shard_map/up/pallas_call | solution.py:236
  66.0 8.0 %down.1 = (bf16[512,768]{1,0:T(8,128)(2,1)}, f32[512,768]{1,0:T(8,128)S(1)}, bf16[512,768]{1,0:T(8,128)(2,1)S(1)}, f32[8,768]{1,0:T(8,128)S(1)}) custom-call(s32[3]{0:T(128)S(1)} %copy-done, bf16[4,512,768]{2,1,0:T(8,128)(2,1)S(1)} %get-tuple-element.162.act.varied, bf16[768,768]{1,0:T(8,128)(2,1)S(1)} %copy-done.2, ...), custom_call_target="tpu_custom_call" | custom-call | flops 28519999488 | bytes 89280000 | tf_op jit(solution)/shard_map/down/pallas_call | solution.py:299
  74.1 4.5 %outer.2 = (bf16[2,768,768]{2,1,0:T(8,128)(2,1)S(1)}, bf16[2,384,768]{2,1,0:T(8,128)(2,1)S(1)}, bf16[2,384,768]{2,1,0:T(8,128)(2,1)S(1)}) custom-call(s32[3]{0:T(128)S(1)} %copy-done, bf16[512,768]{1,0:T(8,128)(2,1)S(1)} %get-tuple-element.165.left.gl, bf16[4,512,768]{2,1,0:T(8,128)(2,1)S(1)} %get-tuple-element.162.act.varied), custom_call_target="tpu_custom_call" | custom-call | flops 25300000768 | bytes 79200000 | tf_op jit(solution)/shard_map/outer/pallas_call | solution.py:469
  78.8 10.8 %back.1 = (bf16[4,512,768]{2,1,0:T(8,128)(2,1)S(1)}, f32[512,768]{1,0:T(8,128)S(1)}, bf16[512,768]{1,0:T(8,128)(2,1)}, f32[16,768]{1,0:T(8,128)S(1)}) custom-call(bf16[512,768]{1,0:T(8,128)(2,1)S(1)} %get-tuple-element.165.left.gl, bf16[4,512,768]{2,1,0:T(8,128)(2,1)S(1)} %copy-done.22, bf16[768,768]{1,0:T(8,128)(2,1)S(1)} %copy-done.2, ...), custom_call_target="tpu_custom_call" | custom-call | flops 49679998976 | bytes 155520000 | tf_op jit(solution)/shard_map/back/pallas_call | solution.py:372
  92.4 4.6 %outer.3 = (bf16[2,768,768]{2,1,0:T(8,128)(2,1)S(1)}, bf16[768,384]{1,0:T(8,128)(2,1)S(1)}, bf16[384,384]{1,0:T(8,128)(2,1)S(1)}, bf16[384,384]{1,0:T(8,128)(2,1...) custom-call(s32[3]{0:T(128)S(1)} %copy-done, bf16[512,768]{1,0:T(8,128)(2,1)S(1)} %copy-done.30, ...), custom_call_target="tpu_custom_call" | custom-call | flops 25300000768 | bytes 79200000 | tf_op jit(solution)/shard_map/outer/pallas_call | solution.py:469
  97.2 10.0 %attend_bwd.3 = (bf16[512,768]{1,0:T(8,128)(2,1)S(1)}, bf16[512,768]{1,0:T(8,128)(2,1)S(1)}, f32[768,768]{1,0:T(8,128)S(1)}, f32[8,768]{1,0:T(8,128)S(1)}) custom-call(s32[3]{0:T(128)S(1)} %copy-done, bf16[2048,768]{1,0:T(8,128)(2,1)} %x_ref.13, bf16[512,768]{1,0:T(8,128)(2,1)} %get-tuple-element.183.rest_0_, ...), custom_call_target="tpu_custom_call" | custom-call | flops 46000001024 | bytes 144000000 | tf_op jit(solution)/shard_map/attend_bwd/pallas_call | solution.py:618
  112.2 5.4 %attend_bwd.4 = (bf16[512,768]{1,0:T(8,128)(2,1)S(1)}, f32[768,768]{1,0:T(8,128)S(1)}, f32[8,768]{1,0:T(8,128)S(1)}) custom-call(s32[3]{0:T(128)S(1)} %copy-done, bf16[2048,768]{1,0:T(8,128)(2,1)} %x_ref.13, bf16[512,768]{1,0:T(8,128)(2,1)S(1)} %collective-permute-done.22.rest_0_, bf16[1,192,512]{2,1,0:T(8,128)(2,1)S(1)} %copy-done.34, ...), custom_call_target="tpu_custom_call" | custom-call | flops 23000000512 | bytes 72000000 | tf_op jit(solution)/shard_map/attend_bwd/pallas_call | solution.py:618
  117.8 5.9 %attend_bwd.5 = (bf16[512,768]{1,0:T(8,128)(2,1)S(1)}, bf16[400,768]{1,0:T(8,128)(2,1)S(1)}, bf16[400,768]{1,0:T(8,128)(2,1)S(1)}) custom-call(s32[3]{0:T(128)S(1)} %copy-done, bf16[2048,768]{1,0:T(8,128)(2,1)} %x_ref.13, bf16[512,768]{1,0:T(8,128)(2,1)S(1)} %collective-permute-done.24.rest_0_, bf16[1,192,512]{2,1,0:T(8,128)(2,1)S(1)} %copy-done.31, ...), custom_call_target="tpu_custom_call" | custom-call | flops 23000000512 | bytes 72000000 | tf_op jit(solution)/shard_map/attend_bwd/pallas_call | solution.py:618
  131.5 8.5 %collective-permute-done.28.refs_1_ = bf16[400,768]{1,0:T(8,128)(2,1)S(1)} collective-permute-done((bf16[400,768]{1,0:T(8,128)(2,1)S(1)}, bf16[400,768]{1,0:T(8,128)(2,1)S(1)}, u32[]{:S(2)}, u32[]{:S(2)}) %collective-permute-start.28) | collective-permute-done | bytes 614432 | tf_op jit(solution)/shard_map/ppermute | solution.py:777
  143.3 4.5 %collective-permute-done.31.refs_7_ = bf16[384,384]{1,0:T(8,128)(2,1)S(1)} collective-permute-done((bf16[384,384]{1,0:T(8,128)(2,1)S(1)}, bf16[384,384]{1,0:T(8,128)(2,1)S(1)}, u32[]{:S(2)}, u32[]{:S(2)}) %collective-permute-start.31) | collective-permute-done | bytes 294944 | tf_op jit(solution)/shard_map/ppermute | solution.py:777
  155.6 8.0 %collective-permute-done.34.refs_1_ = bf16[192,768]{1,0:T(8,128)(2,1)S(1)} collective-permute-done((bf16[192,768]{1,0:T(8,128)(2,1)S(1)}, bf16[192,768]{1,0:T(8,128)(2,1)S(1)}, u32[]{:S(2)}, u32[]{:S(2)}) %collective-permute-start.34) | collective-permute-done | bytes 294944 | tf_op jit(solution)/shard_map/ppermute | solution.py:777
  164.9 3.1 %collective-permute-done.36.refs_1_ = bf16[200,768]{1,0:T(8,128)(2,1)S(1)} collective-permute-done((bf16[200,768]{1,0:T(8,128)(2,1)S(1)}, bf16[200,768]{1,0:T(8,128)(2,1)S(1)}, u32[]{:S(2)}, u32[]{:S(2)}) %collective-permute-start.36) | collective-permute-done | bytes 307232 | tf_op jit(solution)/shard_map/ppermute | solution.py:777
  168.6 3.1 %collective-permute-start.40 = (bf16[192,768]{1,0:T(8,128)(2,1)S(1)}, bf16[192,768]{1,0:T(8,128)(2,1)S(1)}, u32[]{:S(2)}, u32[]{:S(2)}) collective-permute-start(bf16[192,768]{1,0:T(8,128)(2,1)S(1)} %add_up.21.refs_0_), channel_id=1, source_target_pairs={{0,16},{4,20},{8,24},{12,28},{16,0},{20,4},{24,8},{28,12},{1,17},{... | collective-permute-start | bytes 884744 | tf_op jit(solution)/shard_map/ppermute | solution.py:777
  174.4 5.2 %collective-permute-done.39.refs_1_ = bf16[200,768]{1,0:T(8,128)(2,1)S(1)} collective-permute-done((bf16[200,768]{1,0:T(8,128)(2,1)S(1)}, bf16[200,768]{1,0:T(8,128)(2,1)S(1)}, u32[]{:S(2)}, u32[]{:S(2)}) %collective-permute-start.39) | collective-permute-done | bytes 307232 | tf_op jit(solution)/shard_map/ppermute | solution.py:777
  180.2 10.2 %collective-permute-done.40.refs_1_ = bf16[192,768]{1,0:T(8,128)(2,1)S(1)} collective-permute-done((bf16[192,768]{1,0:T(8,128)(2,1)S(1)}, bf16[192,768]{1,0:T(8,128)(2,1)S(1)}, u32[]{:S(2)}, u32[]{:S(2)}) %collective-permute-start.40) | collective-permute-done | bytes 294944 | tf_op jit(solution)/shard_map/ppermute | solution.py:777
  191.1 3.4 %collective-permute-done.41.refs_1_ = bf16[192,768]{1,0:T(8,128)(2,1)S(1)} collective-permute-done((bf16[192,768]{1,0:T(8,128)(2,1)S(1)}, bf16[192,768]{1,0:T(8,128)(2,1)S(1)}, u32[]{:S(2)}, u32[]{:S(2)}) %collective-permute-start.41) | collective-permute-done | bytes 294944 | tf_op jit(solution)/shard_map/ppermute | solution.py:777
  195.6 4.2 %collective-permute-done.42.refs_1_ = bf16[192,768]{1,0:T(8,128)(2,1)S(1)} collective-permute-done((bf16[192,768]{1,0:T(8,128)(2,1)S(1)}, bf16[192,768]{1,0:T(8,128)(2,1)S(1)}, u32[]{:S(2)}, u32[]{:S(2)}) %collective-permute-start.42) | collective-permute-done | bytes 294944 | tf_op jit(solution)/shard_map/ppermute | solution.py:777
  206.4 5.1 %collective-permute-done.46.refs_2_ = bf16[192,768]{1,0:T(8,128)(2,1)S(1)} collective-permute-done((bf16[192,768]{1,0:T(8,128)(2,1)S(1)}, bf16[192,768]{1,0:T(8,128)(2,1)S(1)}, u32[]{:S(2)}, u32[]{:S(2)}) %collective-permute-start.46) | collective-permute-done | bytes 294944 | tf_op jit(solution)/shard_map/ppermute | solution.py:777
  211.5 3.2 %collective-permute-done.47.refs_3_ = bf16[192,768]{1,0:T(8,128)(2,1)S(1)} collective-permute-done((bf16[192,768]{1,0:T(8,128)(2,1)S(1)}, bf16[192,768]{1,0:T(8,128)(2,1)S(1)}, u32[]{:S(2)}, u32[]{:S(2)}) %collective-permute-start.47) | collective-permute-done | bytes 294944 | tf_op jit(solution)/shard_map/ppermute | solution.py:777
  (224 shorter events, 71.1 us)
Async XLA Ops:
  1.3 15.9 %collective-permute-start.6 = (f32[1,768]{1,0:T(1,128)S(1)}, f32[1,768]{1,0:T(1,128)S(1)}, u32[]{:S(2)}, u32[]{:S(2)}) collective-permute-start(f32[1,768]{1,0:T(1,128)S(1)} %reshape.66.b0), channel_id=1, source_target_pairs={{0,2},{1,3},{2,0},{3,1},{4,6},{5,7},{6,4},{7,5},{8,10},{9,11},{10,... | collective-permute-start | bytes 9224 | tf_op jit(solution)/shard_map/ppermute | solution.py:777
  4.3 23.8 %collective-permute-start.3 = (bf16[768,768]{1,0:T(8,128)(2,1)}, bf16[768,768]{1,0:T(8,128)(2,1)S(1)}, u32[]{:S(2)}, u32[]{:S(2)}) collective-permute-start(bf16[768,768]{1,0:T(8,128)(2,1)} %u0.3), channel_id=1, source_target_pairs={{0,1},{1,0},{2,3},{3,2},{4,5},{5,4},{6,7},{7,6},{8,9},{9,8},{10,11... | collective-permute-start | bytes 3538952 | tf_op jit(solution)/shard_map/ppermute | solution.py:777
  8.2 13.9 %collective-permute-start.2 = (bf16[192,768]{1,0:T(8,128)(2,1)}, bf16[192,768]{1,0:T(8,128)(2,1)}, u32[]{:S(2)}, u32[]{:S(2)}) collective-permute-start(bf16[192,768]{1,0:T(8,128)(2,1)} %constant_dynamic-slice_fusion.1), channel_id=1, source_target_pairs={{0,2},{1,3},{2,0},{3,1},{4,6},{5,7},{6,4},{7,5},{8,10},{9,11},{10,... | collective-permute-start | bytes 884744 | tf_op jit(solution)/shard_map/ppermute | solution.py:777
  30.6 20.0 %collective-permute-start.12 = (bf16[512,768]{1,0:T(8,128)(2,1)S(1)}, bf16[512,768]{1,0:T(8,128)(2,1)S(1)}, u32[]{:S(2)}, u32[]{:S(2)}) collective-permute-start(bf16[512,768]{1,0:T(8,128)(2,1)S(1)} %add.21), channel_id=1, source_target_pairs={{0,2},{1,3},{2,0},{3,1},{4,6},{5,7},{6,4},{7,5},{8,10},{9,11},{10,... | collective-permute-start | bytes 2359304 | tf_op jit(solution)/shard_map/ppermute | solution.py:777
  31.1 19.5 %collective-permute-start.13 = (bf16[192,768]{1,0:T(8,128)(2,1)S(1)}, bf16[192,768]{1,0:T(8,128)(2,1)S(1)}, u32[]{:S(2)}, u32[]{:S(2)}) collective-permute-start(bf16[192,768]{1,0:T(8,128)(2,1)S(1)} %collective-permute-done.7.refs_2_), channel_id=1, source_target_pairs={{0,8},{4,12},{8,0},{12,4},{16,24},{20,28},{24,16},{28,20},{1,9},{5... | collective-permute-start | bytes 884744 | tf_op jit(solution)/shard_map/ppermute | solution.py:777
  89.6 20.1 %collective-permute-start.22 = (bf16[512,768]{1,0:T(8,128)(2,1)}, bf16[512,768]{1,0:T(8,128)(2,1)S(1)}, u32[]{:S(2)}, u32[]{:S(2)}) collective-permute-start(bf16[512,768]{1,0:T(8,128)(2,1)} %get-tuple-element.183.rest_0_), channel_id=1, source_target_pairs={{0,2},{1,3},{2,0},{3,1},{4,6},{5,7},{6,4},{7,5},{8,10},{9,11},{10,... | collective-permute-start | bytes 2359304 | tf_op jit(solution)/shard_map/ppermute | solution.py:777
  90.2 19.5 %collective-permute-start.18 = (f32[16,768]{1,0:T(8,128)S(1)}, f32[16,768]{1,0:T(8,128)S(1)}, u32[]{:S(2)}, u32[]{:S(2)}) collective-permute-start(f32[16,768]{1,0:T(8,128)S(1)} %get-tuple-element.173.v), channel_id=1, source_target_pairs={{0,1},{1,0},{2,3},{3,2},{4,5},{5,4},{6,7},{7,6},{8,9},{9,8},{10,11... | collective-permute-start | bytes 147464 | tf_op jit(solution)/shard_map/ppermute | solution.py:777
  90.7 34.7 %collective-permute-start.25 = (bf16[2,384,768]{2,1,0:T(8,128)(2,1)S(1)}, bf16[2,384,768]{2,1,0:T(8,128)(2,1)S(1)}, u32[]{:S(2)}, u32[]{:S(2)}) collective-permute-start(bf16[2,384,768]{2,1,0:T(8,128)(2,1)S(1)} %slice_add_fusion), channel_id=1, source_target_pairs={{0,4},{4,0},{8,12},{12,8},{16,20},{20,16},{24,28},{28,24},{1,5},{5... | collective-permute-start | bytes 3538952 | tf_op jit(solution)/shard_map/ppermute | solution.py:777
  110.2 18.1 %collective-permute-start.27 = (bf16[768,384]{1,0:T(8,128)(2,1)S(1)}, bf16[768,384]{1,0:T(8,128)(2,1)S(1)}, u32[]{:S(2)}, u32[]{:S(2)}) collective-permute-start(bf16[768,384]{1,0:T(8,128)(2,1)S(1)} %bitcast_add_fusion), channel_id=1, source_target_pairs={{0,2},{1,3},{2,0},{3,1},{4,6},{5,7},{6,4},{7,5},{8,10},{9,11},{10,... | collective-permute-start | bytes 1769480 | tf_op jit(solution)/shard_map/ppermute | solution.py:777
  111.8 15.7 %collective-permute-start.26 = (bf16[2,384,384]{2,1,0:T(8,128)(2,1)S(1)}, bf16[2,384,384]{2,1,0:T(8,128)(2,1)S(1)}, u32[]{:S(2)}, u32[]{:S(2)}) collective-permute-start(bf16[2,384,384]{2,1,0:T(8,128)(2,1)S(1)} %slice_add_fusion.1), channel_id=1, source_target_pairs={{0,8},{4,12},{8,0},{12,4},{16,24},{20,28},{24,16},{28,20},{1,9},{5... | collective-permute-start | bytes 1769480 | tf_op jit(solution)/shard_map/ppermute | solution.py:777
  123.7 25.3 %collective-permute-start.32 = (bf16[512,768]{1,0:T(8,128)(2,1)S(1)}, bf16[512,768]{1,0:T(8,128)(2,1)S(1)}, u32[]{:S(2)}, u32[]{:S(2)}) collective-permute-start(bf16[512,768]{1,0:T(8,128)(2,1)S(1)} %get-tuple-element.226), channel_id=1, source_target_pairs={{0,1},{1,0},{2,3},{3,2},{4,5},{5,4},{6,7},{7,6},{8,9},{9,8},{10,11... | collective-permute-start | bytes 2359304 | tf_op jit(solution)/shard_map/ppermute | solution.py:777
  124.0 16.0 %collective-permute-start.28 = (bf16[400,768]{1,0:T(8,128)(2,1)S(1)}, bf16[400,768]{1,0:T(8,128)(2,1)S(1)}, u32[]{:S(2)}, u32[]{:S(2)}) collective-permute-start(bf16[400,768]{1,0:T(8,128)(2,1)S(1)} %get-tuple-element.209), channel_id=1, source_target_pairs={{0,4},{4,0},{8,12},{12,8},{16,20},{20,16},{24,28},{28,24},{1,5},{5... | collective-permute-start | bytes 1843208 | tf_op jit(solution)/shard_map/ppermute | solution.py:777
  126.2 16.3 %collective-permute-start.29 = (bf16[384,768]{1,0:T(8,128)(2,1)S(1)}, bf16[384,768]{1,0:T(8,128)(2,1)S(1)}, u32[]{:S(2)}, u32[]{:S(2)}) collective-permute-start(bf16[384,768]{1,0:T(8,128)(2,1)S(1)} %add_up.13), channel_id=1, source_target_pairs={{0,2},{1,3},{2,0},{3,1},{4,6},{5,7},{6,4},{7,5},{8,10},{9,11},{10,... | collective-permute-start | bytes 1769480 | tf_op jit(solution)/shard_map/ppermute | solution.py:777
  129.0 14.3 %collective-permute-start.30 = (bf16[384,384]{1,0:T(8,128)(2,1)S(1)}, bf16[384,384]{1,0:T(8,128)(2,1)S(1)}, u32[]{:S(2)}, u32[]{:S(2)}) collective-permute-start(bf16[384,384]{1,0:T(8,128)(2,1)S(1)} %add_up.15), channel_id=1, source_target_pairs={{0,8},{4,12},{8,0},{12,4},{16,24},{20,28},{24,16},{28,20},{1,9},{5... | collective-permute-start | bytes 884744 | tf_op jit(solution)/shard_map/ppermute | solution.py:777
  130.0 17.9 %collective-permute-start.31 = (bf16[384,384]{1,0:T(8,128)(2,1)S(1)}, bf16[384,384]{1,0:T(8,128)(2,1)S(1)}, u32[]{:S(2)}, u32[]{:S(2)}) collective-permute-start(bf16[384,384]{1,0:T(8,128)(2,1)S(1)} %add_up.14), channel_id=1, source_target_pairs={{0,2},{1,3},{2,0},{3,1},{4,6},{5,7},{6,4},{7,5},{8,10},{9,11},{10,... | collective-permute-start | bytes 884744 | tf_op jit(solution)/shard_map/ppermute | solution.py:777
  142.5 29.3 %collective-permute-start.37 = (bf16[512,768]{1,0:T(8,128)(2,1)S(1)}, bf16[512,768]{1,0:T(8,128)(2,1)S(1)}, u32[]{:S(2)}, u32[]{:S(2)}) collective-permute-start(bf16[512,768]{1,0:T(8,128)(2,1)S(1)} %get-tuple-element.236), channel_id=1, source_target_pairs={{0,1},{1,0},{2,3},{3,2},{4,5},{5,4},{6,7},{7,6},{8,9},{9,8},{10,11... | collective-permute-start | bytes 2359304 | tf_op jit(solution)/shard_map/ppermute | solution.py:777
  149.7 22.5 %collective-permute-start.38 = (bf16[512,768]{1,0:T(8,128)(2,1)S(1)}, bf16[512,768]{1,0:T(8,128)(2,1)S(1)}, u32[]{:S(2)}, u32[]{:S(2)}) collective-permute-start(bf16[512,768]{1,0:T(8,128)(2,1)S(1)} %add_up.19), channel_id=1, source_target_pairs={{0,2},{1,3},{2,0},{3,1},{4,6},{5,7},{6,4},{7,5},{8,10},{9,11},{10,... | collective-permute-start | bytes 2359304 | tf_op jit(solution)/shard_map/ppermute | solution.py:777
  152.5 15.5 %collective-permute-start.36 = (bf16[200,768]{1,0:T(8,128)(2,1)S(1)}, bf16[200,768]{1,0:T(8,128)(2,1)S(1)}, u32[]{:S(2)}, u32[]{:S(2)}) collective-permute-start(bf16[200,768]{1,0:T(8,128)(2,1)S(1)} %add_up.20.refs_0_), channel_id=1, source_target_pairs={{0,16},{4,20},{8,24},{12,28},{16,0},{20,4},{24,8},{28,12},{1,17},{... | collective-permute-start | bytes 921608 | tf_op jit(solution)/shard_map/ppermute | solution.py:777
  168.6 21.8 %collective-permute-start.40 = (bf16[192,768]{1,0:T(8,128)(2,1)S(1)}, bf16[192,768]{1,0:T(8,128)(2,1)S(1)}, u32[]{:S(2)}, u32[]{:S(2)}) collective-permute-start(bf16[192,768]{1,0:T(8,128)(2,1)S(1)} %add_up.21.refs_0_), channel_id=1, source_target_pairs={{0,16},{4,20},{8,24},{12,28},{16,0},{20,4},{24,8},{28,12},{1,17},{... | collective-permute-start | bytes 884744 | tf_op jit(solution)/shard_map/ppermute | solution.py:777
  171.7 22.8 %collective-permute-start.41 = (bf16[192,768]{1,0:T(8,128)(2,1)S(1)}, bf16[192,768]{1,0:T(8,128)(2,1)S(1)}, u32[]{:S(2)}, u32[]{:S(2)}) collective-permute-start(bf16[192,768]{1,0:T(8,128)(2,1)S(1)} %add_up.22.refs_0_), channel_id=1, source_target_pairs={{0,16},{4,20},{8,24},{12,28},{16,0},{20,4},{24,8},{28,12},{1,17},{... | collective-permute-start | bytes 884744 | tf_op jit(solution)/shard_map/ppermute | solution.py:777
  171.8 28.1 %collective-permute-start.43 = (bf16[200,768]{1,0:T(8,128)(2,1)S(1)}, bf16[200,768]{1,0:T(8,128)(2,1)S(1)}, u32[]{:S(2)}, u32[]{:S(2)}) collective-permute-start(bf16[200,768]{1,0:T(8,128)(2,1)S(1)} %add_up.23.refs_0_), channel_id=1, source_target_pairs={{0,4},{4,0},{8,12},{12,8},{16,20},{20,16},{24,28},{28,24},{1,5},{5... | collective-permute-start | bytes 921608 | tf_op jit(solution)/shard_map/ppermute | solution.py:777
  179.6 22.3 %collective-permute-start.44 = (bf16[200,768]{1,0:T(8,128)(2,1)S(1)}, bf16[200,768]{1,0:T(8,128)(2,1)S(1)}, u32[]{:S(2)}, u32[]{:S(2)}) collective-permute-start(bf16[200,768]{1,0:T(8,128)(2,1)S(1)} %collective-permute-done.39.refs_1_), channel_id=1, source_target_pairs={{0,4},{4,0},{8,12},{12,8},{16,20},{20,16},{24,28},{28,24},{1,5},{5... | collective-permute-start | bytes 921608 | tf_op jit(solution)/shard_map/ppermute | solution.py:777
  195.6 21.1 %collective-permute-start.48 = (bf16[192,768]{1,0:T(8,128)(2,1)S(1)}, bf16[192,768]{1,0:T(8,128)(2,1)S(1)}, u32[]{:S(2)}, u32[]{:S(2)}) collective-permute-start(bf16[192,768]{1,0:T(8,128)(2,1)S(1)} %add_up.25.refs_0_), channel_id=1, source_target_pairs={{0,8},{4,12},{8,0},{12,4},{16,24},{20,28},{24,16},{28,20},{1,9},{5... | collective-permute-start | bytes 884744 | tf_op jit(solution)/shard_map/ppermute | solution.py:777
  199.9 14.8 %collective-permute-start.47 = (bf16[192,768]{1,0:T(8,128)(2,1)S(1)}, bf16[192,768]{1,0:T(8,128)(2,1)S(1)}, u32[]{:S(2)}, u32[]{:S(2)}) collective-permute-start(bf16[192,768]{1,0:T(8,128)(2,1)S(1)} %collective-permute-done.42.refs_1_), channel_id=1, source_target_pairs={{0,4},{4,0},{8,12},{12,8},{16,20},{20,16},{24,28},{28,24},{1,5},{5... | collective-permute-start | bytes 884744 | tf_op jit(solution)/shard_map/ppermute | solution.py:777
  (77 other events, 688.9 us)
where the time goes:
time: 219 us
  Pallas kernels  95.6 us (44%)
  waiting for transfers between devices  73.9 us (34%)
  starting transfers between devices  39.9 us (18%)
  local copies, waits for them, and re-layouts  6.71 us (3%)
    ppermute x50, waiting for transfers between devices, over(): return lambda a: lax.ppermute(a, name, pairs)  73.9 us
    ppermute x50, starting transfers between devices, over(): return lambda a: lax.ppermute(a, name, pairs)  39.9 us
    pallas_call x3, Pallas kernels, attend_bwd(): pl.pallas_call(partial(attend_bwd_kernel, count, later, last), out_shape=...  21.3 us
    pallas_call x3, Pallas kernels, attend_fwd(): pl.pallas_call(partial(attend_fwd_kernel, base), out_shape=saved + (jax.S...  18.4 us
    pallas_call x1, Pallas kernels, back(): pl.pallas_call(back_kernel, out_shape=(jax.ShapeDtypeStruct((4, seq, unit...  10.8 us
    pallas_call x13, Pallas kernels, add_up(): pl.pallas_call(partial(add_up_kernel, tuple((len(part) for part in parts)...  9.24 us
    pallas_call x2, Pallas kernels, outer(): pl.pallas_call(partial(outer_kernel, flip, z_major, halves), out_shape=[j...  9.04 us
    pallas_call x1, Pallas kernels, up(): pl.pallas_call(up_kernel, out_shape=(jax.ShapeDtypeStruct((seq, d), F32),...  8.5 us
  transfers between devices with their start and end apart: 50, of which 17 were waited for; matrix products, arithmetic and copies ran while one was open for 3% of the time, Pallas kernels for 36%

commit v1 on v0

--- a/solution.py
+++ b/solution.py
@@ -186,7 +186,7 @@
     def one(i, c):
         return body(pl.ds(pl.multiple_of(i * step, step), step), c)
 
-    return lax.fori_loop(0, total // step, one, carry, unroll=2)
+    return lax.fori_loop(0, total // step, one, carry, unroll=4)
 
 
 def fold(a):
@@ -949,8 +949,8 @@
         grad_q, grad_k, grad_v, grad_o, vecs = kernel(unpack, False, TAIL, (s_a, q_a, p_a, r_a))
         (q_u,) = wait(q_u)
         r_u = z1(q_u)
+        (grad_up,) = kernel(unpack, True, 0, (s_u, q_u, p_u, r_u))
         (grad_down,) = kernel(unpack, False, 0, (s_d, q_d, p_d, r_d))
-        (grad_up,) = kernel(unpack, True, 0, (s_u, q_u, p_u, r_u))
     else:
         input_grad = finish(idx, in0, from_in1, y(in2 + core(in3)), grad_mid)
         td = jnp.concatenate([first_d[1] + rd[1, :half], second_d[1]]) + y(

time: 219 us -> 217 us (level)
  waiting for transfers between devices: 73.9 us -> 71.7 us
    ppermute x50, waiting for transfers between devices: 73.9 us -> 71.7 us  [over(): return lambda a: lax.ppermute(a, name, pairs)]
  transfers between devices with their start and end apart: 50 -> 50, of which waited for: 17 -> 17; matrix products, arithmetic and copies ran while one was open for 3% -> 3% of each run, Pallas kernels for 36% -> 37%
where the time goes in v1:
time: 217 us; the launch traced here: 216 us
  Pallas kernels  95.4 us (44%)
  waiting for transfers between devices  71.7 us (33%)
  starting transfers between devices  39.9 us (18%)
  local copies, waits for them, and re-layouts  6.71 us (3%)
    ppermute x50, waiting for transfers between devices, over(): return lambda a: lax.ppermute(a, name, pairs)  71.7 us
    ppermute x50, starting transfers between devices, over(): return lambda a: lax.ppermute(a, name, pairs)  39.9 us
    pallas_call x3, Pallas kernels, attend_bwd(): pl.pallas_call(partial(attend_bwd_kernel, count, later, last), out_shape=...  21.1 us
    pallas_call x3, Pallas kernels, attend_fwd(): pl.pallas_call(partial(attend_fwd_kernel, base), out_shape=saved + (jax.S...  18.4 us
    pallas_call x1, Pallas kernels, back(): pl.pallas_call(back_kernel, out_shape=(jax.ShapeDtypeStruct((4, seq, unit...  10.7 us
    pallas_call x2, Pallas kernels, outer(): pl.pallas_call(partial(outer_kernel, flip, z_major, halves), out_shape=[j...  9.28 us
    pallas_call x13, Pallas kernels, add_up(): pl.pallas_call(partial(add_up_kernel, tuple((len(part) for part in parts)...  9.24 us
    pallas_call x1, Pallas kernels, up(): pl.pallas_call(up_kernel, out_shape=(jax.ShapeDtypeStruct((seq, d), F32),...  8.33 us
  transfers between devices with their start and end apart: 50, of which 17 were waited for; matrix products, arithmetic and copies ran while one was open for 3% of the time, Pallas kernels for 37%

profile of v1, /device:TPU:0, one launch (start us, length us, event | category | flops | bytes accessed | tf_op | source)
XLA Modules:
  0.0 216.4 jit_solution(17858589562454587058)
XLA Ops:
  1.3 3.0 %collective-permute-start.6 = (f32[1,768]{1,0:T(1,128)S(1)}, f32[1,768]{1,0:T(1,128)S(1)}, u32[]{:S(2)}, u32[]{:S(2)}) collective-permute-start(f32[1,768]{1,0:T(1,128)S(1)} %reshape.66.b0), channel_id=1, source_target_pairs={{0,2},{1,3},{2,0},{3,1},{4,6},{5,7},{6,4},{7,5},{8,10},{9,11},{10,... | collective-permute-start | bytes 9224 | tf_op jit(solution)/shard_map/ppermute | solution.py:777
  10.9 6.3 %attend_fwd.3 = (bf16[1,192,512]{2,1,0:T(8,128)(2,1)}, bf16[1,512,192]{2,1,0:T(8,128)(2,1)}, bf16[1,192,512]{2,1,0:T(8,128)(2,1)}, bf16[1,3,512,384]{3,2,1,0:T(8...) custom-call(s32[3]{0:T(128)} %pad_add_fusion.idx, bf16[2048,768]{1,0:T(8,128)(2,1)} %x_ref.13, ...), custom_call_target="tpu_custom_call" | custom-call | flops 14720000000 | bytes 46080000 | tf_op jit(solution)/shard_map/attend_fwd/pallas_call | solution.py:158
  23.6 4.5 %attend_fwd.4 = (bf16[1,192,512]{2,1,0:T(8,128)(2,1)S(1)}, bf16[1,512,192]{2,1,0:T(8,128)(2,1)S(1)}, bf16[1,192,512]{2,1,0:T(8,128)(2,1)S(1)}, bf16[1,3,512,384]...) custom-call(s32[3]{0:T(128)S(1)} %copy-done, bf16[2048,768]{1,0:T(8,128)(2,1)} %x_ref.13, ...), custom_call_target="tpu_custom_call" | custom-call | flops 14720000000 | bytes 46080000 | tf_op jit(solution)/shard_map/attend_fwd/pallas_call | solution.py:158
  31.9 7.7 %attend_fwd.5 = (bf16[2,192,512]{2,1,0:T(8,128)(2,1)S(1)}, bf16[2,512,192]{2,1,0:T(8,128)(2,1)S(1)}, bf16[2,192,512]{2,1,0:T(8,128)(2,1)S(1)}, bf16[2,3,512,384]...) custom-call(s32[3]{0:T(128)S(1)} %copy-done, ...), custom_call_target="tpu_custom_call" | custom-call | flops 29440000000 | bytes 92160000 | tf_op jit(solution)/shard_map/attend_fwd/pallas_call | solution.py:158
  42.3 8.3 %collective-permute-done.12.pc = bf16[512,768]{1,0:T(8,128)(2,1)S(1)} collective-permute-done((bf16[512,768]{1,0:T(8,128)(2,1)S(1)}, bf16[512,768]{1,0:T(8,128)(2,1)S(1)}, u32[]{:S(2)}, u32[]{:S(2)}) %collective-permute-start.12) | collective-permute-done | bytes 786464 | tf_op jit(solution)/shard_map/ppermute | solution.py:777
  53.1 3.2 %collective-permute-done.15.pb = bf16[512,768]{1,0:T(8,128)(2,1)S(1)} collective-permute-done((bf16[512,768]{1,0:T(8,128)(2,1)S(1)}, bf16[512,768]{1,0:T(8,128)(2,1)S(1)}, u32[]{:S(2)}, u32[]{:S(2)}) %collective-permute-start.15) | collective-permute-done | bytes 786464 | tf_op jit(solution)/shard_map/ppermute | solution.py:777
  56.4 8.3 %up.1 = (f32[512,768]{1,0:T(8,128)S(1)}, f32[512,768]{1,0:T(8,128)S(1)}, f32[512,128]{1,0:T(8,128)S(1)}, bf16[512,768]{1,0:T(8,128)(2,1)S(1)}, bf16[4,512,768]{2...) custom-call(s32[3]{0:T(128)S(1)} %copy-done, bf16[2048,768]{1,0:T(8,128)(2,1)} %x_ref.13, ...), custom_call_target="tpu_custom_call" | custom-call | flops 33579999232 | bytes 105120000 | tf_op jit(solution)/shard_map/up/pallas_call | solution.py:236
  65.9 8.0 %down.1 = (bf16[512,768]{1,0:T(8,128)(2,1)}, f32[512,768]{1,0:T(8,128)S(1)}, bf16[512,768]{1,0:T(8,128)(2,1)S(1)}, f32[8,768]{1,0:T(8,128)S(1)}) custom-call(s32[3]{0:T(128)S(1)} %copy-done, bf16[4,512,768]{2,1,0:T(8,128)(2,1)S(1)} %get-tuple-element.162.act.varied, bf16[768,768]{1,0:T(8,128)(2,1)S(1)} %copy-done.2, ...), custom_call_target="tpu_custom_call" | custom-call | flops 28519999488 | bytes 89280000 | tf_op jit(solution)/shard_map/down/pallas_call | solution.py:299
  73.9 4.5 %outer.2 = (bf16[2,768,768]{2,1,0:T(8,128)(2,1)S(1)}, bf16[2,384,768]{2,1,0:T(8,128)(2,1)S(1)}, bf16[2,384,768]{2,1,0:T(8,128)(2,1)S(1)}) custom-call(s32[3]{0:T(128)S(1)} %copy-done, bf16[512,768]{1,0:T(8,128)(2,1)S(1)} %get-tuple-element.165.left.gl, bf16[4,512,768]{2,1,0:T(8,128)(2,1)S(1)} %get-tuple-element.162.act.varied), custom_call_target="tpu_custom_call" | custom-call | flops 25300000768 | bytes 79200000 | tf_op jit(solution)/shard_map/outer/pallas_call | solution.py:469
  78.6 10.7 %back.1 = (bf16[4,512,768]{2,1,0:T(8,128)(2,1)S(1)}, f32[512,768]{1,0:T(8,128)S(1)}, bf16[512,768]{1,0:T(8,128)(2,1)}, f32[16,768]{1,0:T(8,128)S(1)}) custom-call(bf16[512,768]{1,0:T(8,128)(2,1)S(1)} %get-tuple-element.165.left.gl, bf16[4,512,768]{2,1,0:T(8,128)(2,1)S(1)} %copy-done.22, bf16[768,768]{1,0:T(8,128)(2,1)S(1)} %copy-done.2, ...), custom_call_target="tpu_custom_call" | custom-call | flops 49679998976 | bytes 155520000 | tf_op jit(solution)/shard_map/back/pallas_call | solution.py:372
  92.1 4.8 %outer.3 = (bf16[2,768,768]{2,1,0:T(8,128)(2,1)S(1)}, bf16[768,384]{1,0:T(8,128)(2,1)S(1)}, bf16[384,384]{1,0:T(8,128)(2,1)S(1)}, bf16[384,384]{1,0:T(8,128)(2,1...) custom-call(s32[3]{0:T(128)S(1)} %copy-done, bf16[512,768]{1,0:T(8,128)(2,1)S(1)} %copy-done.30, ...), custom_call_target="tpu_custom_call" | custom-call | flops 25300000768 | bytes 79200000 | tf_op jit(solution)/shard_map/outer/pallas_call | solution.py:469
  97.1 9.8 %attend_bwd.3 = (bf16[512,768]{1,0:T(8,128)(2,1)S(1)}, bf16[512,768]{1,0:T(8,128)(2,1)S(1)}, f32[768,768]{1,0:T(8,128)S(1)}, f32[8,768]{1,0:T(8,128)S(1)}) custom-call(s32[3]{0:T(128)S(1)} %copy-done, bf16[2048,768]{1,0:T(8,128)(2,1)} %x_ref.13, bf16[512,768]{1,0:T(8,128)(2,1)} %get-tuple-element.183.rest_0_, ...), custom_call_target="tpu_custom_call" | custom-call | flops 46000001024 | bytes 144000000 | tf_op jit(solution)/shard_map/attend_bwd/pallas_call | solution.py:618
  112.0 5.4 %attend_bwd.4 = (bf16[512,768]{1,0:T(8,128)(2,1)S(1)}, f32[768,768]{1,0:T(8,128)S(1)}, f32[8,768]{1,0:T(8,128)S(1)}) custom-call(s32[3]{0:T(128)S(1)} %copy-done, bf16[2048,768]{1,0:T(8,128)(2,1)} %x_ref.13, bf16[512,768]{1,0:T(8,128)(2,1)S(1)} %collective-permute-done.22.rest_0_, bf16[1,192,512]{2,1,0:T(8,128)(2,1)S(1)} %copy-done.34, ...), custom_call_target="tpu_custom_call" | custom-call | flops 23000000512 | bytes 72000000 | tf_op jit(solution)/shard_map/attend_bwd/pallas_call | solution.py:618
  117.5 5.9 %attend_bwd.5 = (bf16[512,768]{1,0:T(8,128)(2,1)S(1)}, bf16[400,768]{1,0:T(8,128)(2,1)S(1)}, bf16[400,768]{1,0:T(8,128)(2,1)S(1)}) custom-call(s32[3]{0:T(128)S(1)} %copy-done, bf16[2048,768]{1,0:T(8,128)(2,1)} %x_ref.13, bf16[512,768]{1,0:T(8,128)(2,1)S(1)} %collective-permute-done.24.rest_0_, bf16[1,192,512]{2,1,0:T(8,128)(2,1)S(1)} %copy-done.31, ...), custom_call_target="tpu_custom_call" | custom-call | flops 23000000512 | bytes 72000000 | tf_op jit(solution)/shard_map/attend_bwd/pallas_call | solution.py:618
  131.2 8.5 %collective-permute-done.28.refs_1_ = bf16[400,768]{1,0:T(8,128)(2,1)S(1)} collective-permute-done((bf16[400,768]{1,0:T(8,128)(2,1)S(1)}, bf16[400,768]{1,0:T(8,128)(2,1)S(1)}, u32[]{:S(2)}, u32[]{:S(2)}) %collective-permute-start.28) | collective-permute-done | bytes 614432 | tf_op jit(solution)/shard_map/ppermute | solution.py:777
  143.1 4.5 %collective-permute-done.31.refs_7_ = bf16[384,384]{1,0:T(8,128)(2,1)S(1)} collective-permute-done((bf16[384,384]{1,0:T(8,128)(2,1)S(1)}, bf16[384,384]{1,0:T(8,128)(2,1)S(1)}, u32[]{:S(2)}, u32[]{:S(2)}) %collective-permute-start.31) | collective-permute-done | bytes 294944 | tf_op jit(solution)/shard_map/ppermute | solution.py:777
  155.4 7.9 %collective-permute-done.34.refs_1_ = bf16[192,768]{1,0:T(8,128)(2,1)S(1)} collective-permute-done((bf16[192,768]{1,0:T(8,128)(2,1)S(1)}, bf16[192,768]{1,0:T(8,128)(2,1)S(1)}, u32[]{:S(2)}, u32[]{:S(2)}) %collective-permute-start.34) | collective-permute-done | bytes 294944 | tf_op jit(solution)/shard_map/ppermute | solution.py:777
  164.6 3.1 %collective-permute-done.36.refs_1_ = bf16[200,768]{1,0:T(8,128)(2,1)S(1)} collective-permute-done((bf16[200,768]{1,0:T(8,128)(2,1)S(1)}, bf16[200,768]{1,0:T(8,128)(2,1)S(1)}, u32[]{:S(2)}, u32[]{:S(2)}) %collective-permute-start.36) | collective-permute-done | bytes 307232 | tf_op jit(solution)/shard_map/ppermute | solution.py:777
  168.4 3.0 %collective-permute-start.40 = (bf16[192,768]{1,0:T(8,128)(2,1)S(1)}, bf16[192,768]{1,0:T(8,128)(2,1)S(1)}, u32[]{:S(2)}, u32[]{:S(2)}) collective-permute-start(bf16[192,768]{1,0:T(8,128)(2,1)S(1)} %add_up.21.refs_0_), channel_id=1, source_target_pairs={{0,16},{4,20},{8,24},{12,28},{16,0},{20,4},{24,8},{28,12},{1,17},{... | collective-permute-start | bytes 884744 | tf_op jit(solution)/shard_map/ppermute | solution.py:777
  174.1 5.3 %collective-permute-done.39.refs_1_ = bf16[200,768]{1,0:T(8,128)(2,1)S(1)} collective-permute-done((bf16[200,768]{1,0:T(8,128)(2,1)S(1)}, bf16[200,768]{1,0:T(8,128)(2,1)S(1)}, u32[]{:S(2)}, u32[]{:S(2)}) %collective-permute-start.39) | collective-permute-done | bytes 307232 | tf_op jit(solution)/shard_map/ppermute | solution.py:777
  180.0 10.2 %collective-permute-done.40.refs_1_ = bf16[192,768]{1,0:T(8,128)(2,1)S(1)} collective-permute-done((bf16[192,768]{1,0:T(8,128)(2,1)S(1)}, bf16[192,768]{1,0:T(8,128)(2,1)S(1)}, u32[]{:S(2)}, u32[]{:S(2)}) %collective-permute-start.40) | collective-permute-done | bytes 294944 | tf_op jit(solution)/shard_map/ppermute | solution.py:777
  190.9 3.3 %collective-permute-done.41.refs_1_ = bf16[192,768]{1,0:T(8,128)(2,1)S(1)} collective-permute-done((bf16[192,768]{1,0:T(8,128)(2,1)S(1)}, bf16[192,768]{1,0:T(8,128)(2,1)S(1)}, u32[]{:S(2)}, u32[]{:S(2)}) %collective-permute-start.41) | collective-permute-done | bytes 294944 | tf_op jit(solution)/shard_map/ppermute | solution.py:777
  195.4 4.2 %collective-permute-done.42.refs_1_ = bf16[192,768]{1,0:T(8,128)(2,1)S(1)} collective-permute-done((bf16[192,768]{1,0:T(8,128)(2,1)S(1)}, bf16[192,768]{1,0:T(8,128)(2,1)S(1)}, u32[]{:S(2)}, u32[]{:S(2)}) %collective-permute-start.42) | collective-permute-done | bytes 294944 | tf_op jit(solution)/shard_map/ppermute | solution.py:777
  206.1 5.5 %collective-permute-done.47.refs_3_ = bf16[192,768]{1,0:T(8,128)(2,1)S(1)} collective-permute-done((bf16[192,768]{1,0:T(8,128)(2,1)S(1)}, bf16[192,768]{1,0:T(8,128)(2,1)S(1)}, u32[]{:S(2)}, u32[]{:S(2)}) %collective-permute-start.47) | collective-permute-done | bytes 294944 | tf_op jit(solution)/shard_map/ppermute | solution.py:777
  (224 shorter events, 68.7 us)
Async XLA Ops:
  1.3 15.9 %collective-permute-start.6 = (f32[1,768]{1,0:T(1,128)S(1)}, f32[1,768]{1,0:T(1,128)S(1)}, u32[]{:S(2)}, u32[]{:S(2)}) collective-permute-start(f32[1,768]{1,0:T(1,128)S(1)} %reshape.66.b0), channel_id=1, source_target_pairs={{0,2},{1,3},{2,0},{3,1},{4,6},{5,7},{6,4},{7,5},{8,10},{9,11},{10,... | collective-permute-start | bytes 9224 | tf_op jit(solution)/shard_map/ppermute | solution.py:777
  4.3 23.8 %collective-permute-start.3 = (bf16[768,768]{1,0:T(8,128)(2,1)}, bf16[768,768]{1,0:T(8,128)(2,1)S(1)}, u32[]{:S(2)}, u32[]{:S(2)}) collective-permute-start(bf16[768,768]{1,0:T(8,128)(2,1)} %u0.3), channel_id=1, source_target_pairs={{0,1},{1,0},{2,3},{3,2},{4,5},{5,4},{6,7},{7,6},{8,9},{9,8},{10,11... | collective-permute-start | bytes 3538952 | tf_op jit(solution)/shard_map/ppermute | solution.py:777
  8.2 13.9 %collective-permute-start.2 = (bf16[192,768]{1,0:T(8,128)(2,1)}, bf16[192,768]{1,0:T(8,128)(2,1)}, u32[]{:S(2)}, u32[]{:S(2)}) collective-permute-start(bf16[192,768]{1,0:T(8,128)(2,1)} %constant_dynamic-slice_fusion.1), channel_id=1, source_target_pairs={{0,2},{1,3},{2,0},{3,1},{4,6},{5,7},{6,4},{7,5},{8,10},{9,11},{10,... | collective-permute-start | bytes 884744 | tf_op jit(solution)/shard_map/ppermute | solution.py:777
  30.6 20.0 %collective-permute-start.12 = (bf16[512,768]{1,0:T(8,128)(2,1)S(1)}, bf16[512,768]{1,0:T(8,128)(2,1)S(1)}, u32[]{:S(2)}, u32[]{:S(2)}) collective-permute-start(bf16[512,768]{1,0:T(8,128)(2,1)S(1)} %add.21), channel_id=1, source_target_pairs={{0,2},{1,3},{2,0},{3,1},{4,6},{5,7},{6,4},{7,5},{8,10},{9,11},{10,... | collective-permute-start | bytes 2359304 | tf_op jit(solution)/shard_map/ppermute | solution.py:777
  31.1 19.5 %collective-permute-start.13 = (bf16[192,768]{1,0:T(8,128)(2,1)S(1)}, bf16[192,768]{1,0:T(8,128)(2,1)S(1)}, u32[]{:S(2)}, u32[]{:S(2)}) collective-permute-start(bf16[192,768]{1,0:T(8,128)(2,1)S(1)} %collective-permute-done.7.refs_2_), channel_id=1, source_target_pairs={{0,8},{4,12},{8,0},{12,4},{16,24},{20,28},{24,16},{28,20},{1,9},{5... | collective-permute-start | bytes 884744 | tf_op jit(solution)/shard_map/ppermute | solution.py:777
  89.3 20.0 %collective-permute-start.22 = (bf16[512,768]{1,0:T(8,128)(2,1)}, bf16[512,768]{1,0:T(8,128)(2,1)S(1)}, u32[]{:S(2)}, u32[]{:S(2)}) collective-permute-start(bf16[512,768]{1,0:T(8,128)(2,1)} %get-tuple-element.183.rest_0_), channel_id=1, source_target_pairs={{0,2},{1,3},{2,0},{3,1},{4,6},{5,7},{6,4},{7,5},{8,10},{9,11},{10,... | collective-permute-start | bytes 2359304 | tf_op jit(solution)/shard_map/ppermute | solution.py:777
  89.9 19.4 %collective-permute-start.18 = (f32[16,768]{1,0:T(8,128)S(1)}, f32[16,768]{1,0:T(8,128)S(1)}, u32[]{:S(2)}, u32[]{:S(2)}) collective-permute-start(f32[16,768]{1,0:T(8,128)S(1)} %get-tuple-element.173.v), channel_id=1, source_target_pairs={{0,1},{1,0},{2,3},{3,2},{4,5},{5,4},{6,7},{7,6},{8,9},{9,8},{10,11... | collective-permute-start | bytes 147464 | tf_op jit(solution)/shard_map/ppermute | solution.py:777
  90.4 34.8 %collective-permute-start.25 = (bf16[2,384,768]{2,1,0:T(8,128)(2,1)S(1)}, bf16[2,384,768]{2,1,0:T(8,128)(2,1)S(1)}, u32[]{:S(2)}, u32[]{:S(2)}) collective-permute-start(bf16[2,384,768]{2,1,0:T(8,128)(2,1)S(1)} %slice_add_fusion), channel_id=1, source_target_pairs={{0,4},{4,0},{8,12},{12,8},{16,20},{20,16},{24,28},{28,24},{1,5},{5... | collective-permute-start | bytes 3538952 | tf_op jit(solution)/shard_map/ppermute | solution.py:777
  109.9 18.0 %collective-permute-start.27 = (bf16[768,384]{1,0:T(8,128)(2,1)S(1)}, bf16[768,384]{1,0:T(8,128)(2,1)S(1)}, u32[]{:S(2)}, u32[]{:S(2)}) collective-permute-start(bf16[768,384]{1,0:T(8,128)(2,1)S(1)} %bitcast_add_fusion), channel_id=1, source_target_pairs={{0,2},{1,3},{2,0},{3,1},{4,6},{5,7},{6,4},{7,5},{8,10},{9,11},{10,... | collective-permute-start | bytes 1769480 | tf_op jit(solution)/shard_map/ppermute | solution.py:777
  111.5 15.7 %collective-permute-start.26 = (bf16[2,384,384]{2,1,0:T(8,128)(2,1)S(1)}, bf16[2,384,384]{2,1,0:T(8,128)(2,1)S(1)}, u32[]{:S(2)}, u32[]{:S(2)}) collective-permute-start(bf16[2,384,384]{2,1,0:T(8,128)(2,1)S(1)} %slice_add_fusion.1), channel_id=1, source_target_pairs={{0,8},{4,12},{8,0},{12,4},{16,24},{20,28},{24,16},{28,20},{1,9},{5... | collective-permute-start | bytes 1769480 | tf_op jit(solution)/shard_map/ppermute | solution.py:777
  123.4 25.3 %collective-permute-start.32 = (bf16[512,768]{1,0:T(8,128)(2,1)S(1)}, bf16[512,768]{1,0:T(8,128)(2,1)S(1)}, u32[]{:S(2)}, u32[]{:S(2)}) collective-permute-start(bf16[512,768]{1,0:T(8,128)(2,1)S(1)} %get-tuple-element.226), channel_id=1, source_target_pairs={{0,1},{1,0},{2,3},{3,2},{4,5},{5,4},{6,7},{7,6},{8,9},{9,8},{10,11... | collective-permute-start | bytes 2359304 | tf_op jit(solution)/shard_map/ppermute | solution.py:777
  123.7 16.0 %collective-permute-start.28 = (bf16[400,768]{1,0:T(8,128)(2,1)S(1)}, bf16[400,768]{1,0:T(8,128)(2,1)S(1)}, u32[]{:S(2)}, u32[]{:S(2)}) collective-permute-start(bf16[400,768]{1,0:T(8,128)(2,1)S(1)} %get-tuple-element.209), channel_id=1, source_target_pairs={{0,4},{4,0},{8,12},{12,8},{16,20},{20,16},{24,28},{28,24},{1,5},{5... | collective-permute-start | bytes 1843208 | tf_op jit(solution)/shard_map/ppermute | solution.py:777
  126.0 16.3 %collective-permute-start.29 = (bf16[384,768]{1,0:T(8,128)(2,1)S(1)}, bf16[384,768]{1,0:T(8,128)(2,1)S(1)}, u32[]{:S(2)}, u32[]{:S(2)}) collective-permute-start(bf16[384,768]{1,0:T(8,128)(2,1)S(1)} %add_up.13), channel_id=1, source_target_pairs={{0,2},{1,3},{2,0},{3,1},{4,6},{5,7},{6,4},{7,5},{8,10},{9,11},{10,... | collective-permute-start | bytes 1769480 | tf_op jit(solution)/shard_map/ppermute | solution.py:777
  128.7 14.4 %collective-permute-start.30 = (bf16[384,384]{1,0:T(8,128)(2,1)S(1)}, bf16[384,384]{1,0:T(8,128)(2,1)S(1)}, u32[]{:S(2)}, u32[]{:S(2)}) collective-permute-start(bf16[384,384]{1,0:T(8,128)(2,1)S(1)} %add_up.15), channel_id=1, source_target_pairs={{0,8},{4,12},{8,0},{12,4},{16,24},{20,28},{24,16},{28,20},{1,9},{5... | collective-permute-start | bytes 884744 | tf_op jit(solution)/shard_map/ppermute | solution.py:777
  129.7 17.9 %collective-permute-start.31 = (bf16[384,384]{1,0:T(8,128)(2,1)S(1)}, bf16[384,384]{1,0:T(8,128)(2,1)S(1)}, u32[]{:S(2)}, u32[]{:S(2)}) collective-permute-start(bf16[384,384]{1,0:T(8,128)(2,1)S(1)} %add_up.14), channel_id=1, source_target_pairs={{0,2},{1,3},{2,0},{3,1},{4,6},{5,7},{6,4},{7,5},{8,10},{9,11},{10,... | collective-permute-start | bytes 884744 | tf_op jit(solution)/shard_map/ppermute | solution.py:777
  142.2 29.2 %collective-permute-start.37 = (bf16[512,768]{1,0:T(8,128)(2,1)S(1)}, bf16[512,768]{1,0:T(8,128)(2,1)S(1)}, u32[]{:S(2)}, u32[]{:S(2)}) collective-permute-start(bf16[512,768]{1,0:T(8,128)(2,1)S(1)} %get-tuple-element.236), channel_id=1, source_target_pairs={{0,1},{1,0},{2,3},{3,2},{4,5},{5,4},{6,7},{7,6},{8,9},{9,8},{10,11... | collective-permute-start | bytes 2359304 | tf_op jit(solution)/shard_map/ppermute | solution.py:777
  149.4 22.5 %collective-permute-start.38 = (bf16[512,768]{1,0:T(8,128)(2,1)S(1)}, bf16[512,768]{1,0:T(8,128)(2,1)S(1)}, u32[]{:S(2)}, u32[]{:S(2)}) collective-permute-start(bf16[512,768]{1,0:T(8,128)(2,1)S(1)} %add_up.19), channel_id=1, source_target_pairs={{0,2},{1,3},{2,0},{3,1},{4,6},{5,7},{6,4},{7,5},{8,10},{9,11},{10,... | collective-permute-start | bytes 2359304 | tf_op jit(solution)/shard_map/ppermute | solution.py:777
  152.2 15.5 %collective-permute-start.36 = (bf16[200,768]{1,0:T(8,128)(2,1)S(1)}, bf16[200,768]{1,0:T(8,128)(2,1)S(1)}, u32[]{:S(2)}, u32[]{:S(2)}) collective-permute-start(bf16[200,768]{1,0:T(8,128)(2,1)S(1)} %add_up.20.refs_0_), channel_id=1, source_target_pairs={{0,16},{4,20},{8,24},{12,28},{16,0},{20,4},{24,8},{28,12},{1,17},{... | collective-permute-start | bytes 921608 | tf_op jit(solution)/shard_map/ppermute | solution.py:777
  168.4 21.8 %collective-permute-start.40 = (bf16[192,768]{1,0:T(8,128)(2,1)S(1)}, bf16[192,768]{1,0:T(8,128)(2,1)S(1)}, u32[]{:S(2)}, u32[]{:S(2)}) collective-permute-start(bf16[192,768]{1,0:T(8,128)(2,1)S(1)} %add_up.21.refs_0_), channel_id=1, source_target_pairs={{0,16},{4,20},{8,24},{12,28},{16,0},{20,4},{24,8},{28,12},{1,17},{... | collective-permute-start | bytes 884744 | tf_op jit(solution)/shard_map/ppermute | solution.py:777
  171.4 22.8 %collective-permute-start.41 = (bf16[192,768]{1,0:T(8,128)(2,1)S(1)}, bf16[192,768]{1,0:T(8,128)(2,1)S(1)}, u32[]{:S(2)}, u32[]{:S(2)}) collective-permute-start(bf16[192,768]{1,0:T(8,128)(2,1)S(1)} %add_up.22.refs_0_), channel_id=1, source_target_pairs={{0,16},{4,20},{8,24},{12,28},{16,0},{20,4},{24,8},{28,12},{1,17},{... | collective-permute-start | bytes 884744 | tf_op jit(solution)/shard_map/ppermute | solution.py:777
  171.4 28.2 %collective-permute-start.43 = (bf16[200,768]{1,0:T(8,128)(2,1)S(1)}, bf16[200,768]{1,0:T(8,128)(2,1)S(1)}, u32[]{:S(2)}, u32[]{:S(2)}) collective-permute-start(bf16[200,768]{1,0:T(8,128)(2,1)S(1)} %add_up.23.refs_0_), channel_id=1, source_target_pairs={{0,4},{4,0},{8,12},{12,8},{16,20},{20,16},{24,28},{28,24},{1,5},{5... | collective-permute-start | bytes 921608 | tf_op jit(solution)/shard_map/ppermute | solution.py:777
  179.4 22.2 %collective-permute-start.44 = (bf16[200,768]{1,0:T(8,128)(2,1)S(1)}, bf16[200,768]{1,0:T(8,128)(2,1)S(1)}, u32[]{:S(2)}, u32[]{:S(2)}) collective-permute-start(bf16[200,768]{1,0:T(8,128)(2,1)S(1)} %collective-permute-done.39.refs_1_), channel_id=1, source_target_pairs={{0,4},{4,0},{8,12},{12,8},{16,20},{20,16},{24,28},{28,24},{1,5},{5... | collective-permute-start | bytes 921608 | tf_op jit(solution)/shard_map/ppermute | solution.py:777
  199.6 14.0 %collective-permute-start.48 = (bf16[192,768]{1,0:T(8,128)(2,1)S(1)}, bf16[192,768]{1,0:T(8,128)(2,1)S(1)}, u32[]{:S(2)}, u32[]{:S(2)}) collective-permute-start(bf16[192,768]{1,0:T(8,128)(2,1)S(1)} %add_up.24.refs_0_), channel_id=1, source_target_pairs={{0,4},{4,0},{8,12},{12,8},{16,20},{20,16},{24,28},{28,24},{1,5},{5... | collective-permute-start | bytes 884744 | tf_op jit(solution)/shard_map/ppermute | solution.py:777
  199.6 14.6 %collective-permute-start.49 = (bf16[192,768]{1,0:T(8,128)(2,1)S(1)}, bf16[192,768]{1,0:T(8,128)(2,1)S(1)}, u32[]{:S(2)}, u32[]{:S(2)}) collective-permute-start(bf16[192,768]{1,0:T(8,128)(2,1)S(1)} %collective-permute-done.42.refs_1_), channel_id=1, source_target_pairs={{0,4},{4,0},{8,12},{12,8},{16,20},{20,16},{24,28},{28,24},{1,5},{5... | collective-permute-start | bytes 884744 | tf_op jit(solution)/shard_map/ppermute | solution.py:777
  (77 other events, 684.8 us)
